TPU v7x, 256 devices: a whole 4x4x8 slice. The times are simulated.
256 devices in a mesh: src: 16 (over z_lo, y), tgt: 16 (over x, z_hi, core).
Axes of the slice: x: 4, y: 4, z: 8 (z_hi: 2, z_lo: 4; z = z_hi * 4 + z_lo), core: 2. Of those that a mesh axis runs over, the one named last changes fastest.
Arguments:
- signals: float32 [64, 786432], P(None, ('src', 'tgt')), may hold values from -6 to 6
- leaf_maps: float32 [6144, 64, 128], P(('src', 'tgt')), may hold values from -0.5 to 0.5
- root_maps: float32 [6144, 128, 64], P(('src', 'tgt')), may hold values from -0.75 to 0.75
- translations: float32 [8, 8, 64, 64], replicated, may hold values from -0.375 to 0.375
- source_list: int32 [8, 24, 4], replicated, may hold values from 0 to 47, as said below
- type_list: int32 [8, 24, 4], replicated, may hold values from 0 to 7
Outputs:
- focused: float32 [64, 786432], P(None, ('src', 'tgt'))
Inputs may be any that keep to these rules, and one draw needn't show every extreme that they name: `source_list`: entries e < 2 name one of the device's own blocks (below 24); the other entries name one of the partner's blocks (at or above 24).
All inputs are finite; a program needn't handle non-finite values.
Results may differ from a plain program's by a relative error of at most 0.00011.
Values sent between devices are 32-bit elements; how exact they have to be, the bound alone decides.
No kernel may reach another device: no remote copies, remote signals or barrier semaphores. Data moves between devices by JAX's collectives and lax.ppermute only.
A program may use at most 64 MiB of HBM per device.

v0:
```python
import functools

import jax
import jax.numpy as jnp
from jax import lax
from jax.experimental import pallas as pl
from jax.experimental.pallas import tpu as pltpu
from jax.sharding import Mesh, PartitionSpec as P

BITS = ("z1", "z0", "y1", "y0", "x1", "x0", "zh", "c")
GROUP = ("z1", "z0", "y1", "x1", "x0", "zh")
FLIPS = ("y0", "y1", "z0", "z1", "c", "zh", "x0", "x1")
LANES = 128
F32, BF16 = jnp.float32, jnp.bfloat16
NT = (((1,), (1,)), ((), ()))


def row_mask(level):
    return 1 << (len(GROUP) - 1 - GROUP.index(FLIPS[level]))


def dot_nt(a, b):
    return lax.dot_general(a, b, NT, preferred_element_type=F32)


def split(x):
    hi = x.astype(BF16)
    return hi, (x - hi.astype(F32)).astype(BF16)


def low_lanes(shape):
    return lax.broadcasted_iota(jnp.int32, shape, 1) < LANES // 2


def turn(x):
    return pltpu.roll(x, LANES // 2, 1)


def hi_lo_lanes(x):
    hi = x.astype(BF16).astype(F32)
    return jnp.where(low_lanes(x.shape), hi, x - hi).astype(BF16)


def flip_rows(v, mask):
    groups = [v[8 * i : 8 * i + 8] for i in range(v.shape[0] // 8)]
    if mask >= 8:
        groups = [groups[i ^ (mask // 8)] for i in range(len(groups))]
    elif mask == 4:
        groups = [pltpu.roll(g, 4, 0) for g in groups]
    else:
        bit = (lax.broadcasted_iota(jnp.int32, (8, LANES), 0) & mask) != 0
        groups = [jnp.where(bit, pltpu.roll(g, mask, 0), pltpu.roll(g, 8 - mask, 0)) for g in groups]
    return jnp.concatenate(groups, axis=0)


def pair_rows(ref, pair):
    return pl.ds(pair, ref.shape[0] // 12, stride=12)


def put_pair(held, pair, x):
    turned = turn(x)
    low = low_lanes(x.shape)
    held[2 * pair] = hi_lo_lanes(jnp.where(low, x, turned))
    held[2 * pair + 1] = hi_lo_lanes(jnp.where(low, turned, x))


def put_weights(mat, out_ref):
    hi, lo = split(mat.T)
    both = jnp.concatenate([hi, lo], axis=1)
    rank = mat.shape[0]
    out_ref[:rank] = both
    out_ref[rank:] = both


def two_terms(level, block, entry, sources, types, back, held, weights):
    left = [held[sources[level, entry + i, block] - back] for i in range(2)]
    right = [weights[types[level, entry + i, block]] for i in range(2)]
    return jnp.dot(jnp.concatenate(left, axis=1), jnp.concatenate(right, axis=0), preferred_element_type=F32)


def level_step(level, sources, types, held, weights, emit):
    blocks = held.shape[0]

    def pair_step(pair, carry):
        terms = []
        for block in (2 * pair, 2 * pair + 1):
            terms.append(two_terms(level, block, 0, sources, types, 0, held, weights))
            terms.append(two_terms(level, block, 2, sources, types, blocks, held, weights))
        emit(pair, *terms)
        return carry

    lax.fori_loop(0, blocks // 2, pair_step, 0, unroll=6)


def flip_and_keep(held, mask):
    def emit(pair, own_even, other_even, own_odd, other_odd):
        for block, own, other in ((2 * pair, own_even, other_even), (2 * pair + 1, own_odd, other_odd)):
            total = own + flip_rows(other, mask)
            held[block] = hi_lo_lanes(total + turn(total))

    return emit


def flip_and_give(out_ref, mask):
    def emit(pair, own_even, other_even, own_odd, other_odd):
        even = own_even + flip_rows(other_even, mask)
        odd = own_odd + flip_rows(other_odd, mask)
        out_ref[pair_rows(out_ref, pair), :] = join(even, odd)

    return emit


def join(even, odd):
    low = low_lanes(even.shape)
    return jnp.where(low, even, odd) + turn(jnp.where(low, odd, even))


def give_both(own_ref, other_ref):
    def emit(pair, own_even, other_even, own_odd, other_odd):
        own_ref[pair_rows(own_ref, pair), :] = join(own_even, own_odd)
        other_ref[pair_rows(other_ref, pair), :] = join(other_even, other_odd)

    return emit


def run_levels(first, count, sources, types, held, weights, last):
    for i in range(count):
        now, then = held[i % 2], held[(i + 1) % 2]
        emit = last if i == count - 1 else flip_and_keep(then, row_mask(first + i))
        level_step(first + i, sources, types, now, weights.at[first + i - 1], emit)


def start_kernel(
    sources, types, tables, signals, maps, own_ref, other_ref, held, weights, table_in, signals_in, maps_in, sems
):
    blocks, rank, width = maps.shape
    parts = sems.shape[1]
    some = blocks // parts
    table_copy = pltpu.make_async_copy(tables.at[0], table_in, sems.at[2, 0])
    table_copy.start()
    copies = []
    for i in range(parts):
        lanes, rows = pl.ds(i * some * width, some * width), pl.ds(i * some, some)
        copies.append(
            (
                pltpu.make_async_copy(signals.at[:, lanes], signals_in.at[:, lanes], sems.at[0, i]),
                pltpu.make_async_copy(maps.at[rows], maps_in.at[rows], sems.at[1, i]),
            )
        )
        for copy in copies[-1]:
            copy.start()
    table_copy.wait()
    for kind in range(weights.shape[0]):
        put_weights(table_in[kind], weights.at[kind])

    def leaf(k, carry):
        wave_hi, wave_lo = split(signals_in[:, pl.ds(pl.multiple_of(k * width, width), width)])
        map_hi, map_lo = split(maps_in[k])
        left = jnp.concatenate([wave_hi, wave_lo], axis=1)
        both = jnp.concatenate([map_hi, map_lo], axis=0)
        total = dot_nt(left, jnp.concatenate([both, both], axis=1))
        held[k] = hi_lo_lanes(total + turn(total))
        return carry

    for i in range(parts):
        for copy in copies[i]:
            copy.wait()
        lax.fori_loop(i * some, (i + 1) * some, leaf, 0, unroll=some)
    level_step(0, sources, types, held, weights, give_both(own_ref, other_ref))


def prepare_kernel(tables, maps, weights, root_weights):
    def table(level, carry):
        for kind in range(tables.shape[1]):
            put_weights(tables[level + 1, kind], weights.at[level, kind])
        return carry

    lax.fori_loop(0, tables.shape[0] - 1, table, 0)

    def root(block, carry):
        hi, lo = split(maps[block])
        root_weights[block] = jnp.concatenate([hi, hi, lo, lo], axis=0)
        return carry

    lax.fori_loop(0, maps.shape[0], root, 0, unroll=4)


def middle_kernel(sources, types, weights, x_ref, own_ref, other_ref, held, held_too):
    for pair in range(held.shape[0] // 2):
        put_pair(held, pair, x_ref[pair_rows(x_ref, pair), :])
    run_levels(1, 4, sources, types, (held, held_too), weights, give_both(own_ref, other_ref))


def end_kernel(sources, types, weights, own_ref, other_ref, out_ref, held, held_too):
    for pair in range(held.shape[0] // 2):
        rows = pair_rows(own_ref, pair)
        put_pair(held, pair, own_ref[rows, :] + other_ref[rows, :])
    run_levels(5, 3, sources, types, (held, held_too), weights, flip_and_give(out_ref, row_mask(7)))


def root_kernel(x_ref, weights, out_ref):
    blocks, width = weights.shape[0], weights.shape[2]

    def body(pair, carry):
        x = x_ref[pair_rows(x_ref, pair), :]
        turned = turn(x)
        low = low_lanes(x.shape)
        for block, value in ((2 * pair, jnp.where(low, x, turned)), (2 * pair + 1, jnp.where(low, turned, x))):
            left = hi_lo_lanes(value)
            out = jnp.dot(jnp.concatenate([left, left], axis=1), weights[block], preferred_element_type=F32)
            out_ref[:, pl.ds(pl.multiple_of(block * width, width), width)] = out
        return carry

    lax.fori_loop(0, blocks // 2, body, 0, unroll=4)


VMEM = pl.BlockSpec(memory_space=pltpu.VMEM)
SMEM = pl.BlockSpec(memory_space=pltpu.SMEM)
HBM = pl.BlockSpec(memory_space=pltpu.HBM)


def call(kernel, outs, specs, scratch=(), mib=12, cost=None):
    return pl.pallas_call(
        kernel,
        out_shape=outs,
        grid=(1,),
        in_specs=specs,
        out_specs=[VMEM] * len(outs),
        scratch_shapes=scratch,
        cost_estimate=cost,
        compiler_params=pltpu.CompilerParams(vmem_limit_bytes=mib * 2**20),
    )


def exchange(x):
    rows = x.shape[0]
    x = x.reshape(64, 1, rows * LANES // 64)
    return lax.all_to_all(x, GROUP, 0, 0, tiled=True).reshape(rows, LANES)


def partner(x, axis):
    return lax.ppermute(x, axis, [(0, 1), (1, 0)])


def local(signals, leaf_maps, root_maps, translations, source_list, type_list):
    blocks, rank, width = leaf_maps.shape
    waves = signals.shape[0]
    levels, kinds = translations.shape[:2]
    sources, types = jnp.swapaxes(source_list, 1, 2), jnp.swapaxes(type_list, 1, 2)
    root_maps = jnp.swapaxes(root_maps, 1, 2)
    held = pltpu.VMEM((blocks, waves, LANES), BF16)
    flat = jax.ShapeDtypeStruct((waves * blocks // 2, LANES), F32)
    own, other = call(
        start_kernel,
        [flat, flat],
        [SMEM, SMEM, HBM, HBM, HBM],
        [
            held,
            pltpu.VMEM((kinds, 2 * rank, LANES), BF16),
            pltpu.VMEM((kinds, rank, rank), F32),
            pltpu.VMEM((waves, blocks * width), F32),
            pltpu.VMEM((blocks, rank, width), F32),
            pltpu.SemaphoreType.DMA((3, 3)),
        ],
        mib=60,
    )(sources, types, translations, signals, leaf_maps)
    received = partner(other, "y0")
    weights, root_weights = call(
        prepare_kernel,
        [
            jax.ShapeDtypeStruct((levels - 1, kinds, 2 * rank, LANES), BF16),
            jax.ShapeDtypeStruct((blocks, 4 * rank, width), BF16),
        ],
        [VMEM, VMEM],
        cost=pl.CostEstimate(flops=2**24, bytes_accessed=2**23, transcendentals=0),
    )(translations, root_maps)
    x, weights, root_weights = lax.optimization_barrier((own + received, weights, root_weights))
    x = exchange(x)
    own, other = call(middle_kernel, [flat, flat], [SMEM, SMEM, VMEM, VMEM], [held, held])(sources, types, weights, x)
    (x,) = call(end_kernel, [flat], [SMEM, SMEM, VMEM, VMEM, VMEM], [held, held])(
        sources, types, weights, own, partner(other, "c")
    )
    (out,) = call(root_kernel, [jax.ShapeDtypeStruct((waves, blocks * width), F32)], [VMEM, VMEM])(
        exchange(x), root_weights
    )
    return out


def solution(mesh):
    fine = Mesh(mesh.devices.reshape((2,) * len(BITS)), BITS)
    placed = (P(None, BITS), P(BITS, None, None), P(BITS, None, None), P(), P(), P())
    return jax.shard_map(local, mesh=fine, in_specs=placed, out_specs=P(None, BITS), check_vma=False)
```

profile of v0, /device:TPU:1, one launch (start us, length us, event | category | flops | bytes accessed | tf_op | source)
XLA Modules:
  0.0 82.0 jit_solution(8230209603797006778)
XLA Ops:
  0.0 0.0 copy-start
  0.0 0.0 copy-start.1
  0.0 5.6 %shard_map.64 = (f32[768,128]{1,0:T(8,128)}, f32[768,128]{1,0:T(8,128)}) custom-call(s32[8,4,24]{2,1,0:T(4,128)} %bitcast.11, s32[8,4,24]{2,1,0:T(4,128)} %bitcast.14, f32[8,8,64,64]{3,2,1,0:T(8,128)} %tables.3, f32[64,3072]{1,0:T(8,128)} %signals.1, f32[24,64,128]{2,1,0:T(8,128)} %maps.1), custom_call_target="tpu_custom_call" | custom-call | tf_op jit(solution)/shard_map/pallas_call | solution.py:253
  5.6 0.0 copy-start.4
  5.6 2.2 %collective-permute-start = (f32[768,128]{1,0:T(8,128)}, f32[768,128]{1,0:T(8,128)S(1)}, u32[]{:S(2)}, u32[]{:S(2)}) collective-permute-start(f32[768,128]{1,0:T(8,128)} %get-tuple-element.15), channel_id=1, source_target_pairs={{0,16},{16,0},{1,17},{17,1},{2,18},{18,2},{3,19},{19,3},{4,20},{20... | collective-permute-start | bytes 1179656 | tf_op jit(solution)/shard_map/ppermute | solution.py:242
  7.8 0.0 copy-done
  7.8 0.0 copy-done.1
  7.8 0.0 copy-start.2
  7.8 0.0 copy-start.3
  7.8 1.6 %shard_map.65 = (bf16[7,8,128,128]{3,2,1,0:T(8,128)(2,1)S(1)}, bf16[24,256,128]{2,1,0:T(8,128)(2,1)S(1)}) custom-call(f32[8,8,64,64]{3,2,1,0:T(8,128)S(1)} %copy-done, f32[24,64,128]{2,1,0:T(8,128)S(1)} %bitcast.10), custom_call_target="tpu_custom_call" | custom-call | flops 16777216 | bytes 8388608 | tf_op jit(solution)/shard_map/pallas_call | solution.py:268
  9.5 6.3 %collective-permute-done = f32[768,128]{1,0:T(8,128)S(1)} collective-permute-done((f32[768,128]{1,0:T(8,128)}, f32[768,128]{1,0:T(8,128)S(1)}, u32[]{:S(2)}, u32[]{:S(2)}) %collective-permute-start) | collective-permute-done | bytes 393248 | tf_op jit(solution)/shard_map/ppermute | solution.py:242
  15.8 0.0 copy-done.4
  15.8 29.3 %all_to_all.10 = f32[64,1,1536]{2,1,0:T(1,128)S(1)} all-to-all(f32[64,1,1536]{2,1,0:T(1,128)S(1)} %bitcast.17), channel_id=1, replica_groups=mesh['z1'=2,'z0'=2,'y1'=2,'y0'=2,'x1'=2,'x0'=2,'zh'=2,'c'=2] {'z1','z0',..., dimensions={0} | all-to-all | bytes 786432 | tf_op jit(solution)/shard_map/all_to_all | solution.py:238
  45.1 0.0 copy-done.2
  45.1 0.0 copy-done.3
  45.1 5.4 %shard_map.66 = (f32[768,128]{1,0:T(8,128)S(1)}, f32[768,128]{1,0:T(8,128)S(1)}) custom-call(s32[8,4,24]{2,1,0:T(4,128)S(1)} %bitcast.12, s32[8,4,24]{2,1,0:T(4,128)S(1)} %bitcast.15, bf16[7,8,128,128]{3,2,1,0:T(8,128)(2,1)S(1)} %get-tuple-element.18.weights, f32[768,128]{1,0:T(8,128)S(1)} %bitcast.8), custom_call_target="tpu_custom_call" | custom-call | tf_op jit(solution)/shard_map/pallas_call | solution.py:279
  50.5 3.5 %collective-permute-start.1 = (f32[768,128]{1,0:T(8,128)S(1)}, f32[768,128]{1,0:T(8,128)S(1)}, u32[]{:S(2)}, u32[]{:S(2)}) collective-permute-start(f32[768,128]{1,0:T(8,128)S(1)} %get-tuple-element.21), channel_id=1, source_target_pairs={{0,1},{1,0},{2,3},{3,2},{4,5},{5,4},{6,7},{7,6},{8,9},{9,8},{10,11... | collective-permute-start | bytes 1179656 | tf_op jit(solution)/shard_map/ppermute | solution.py:242
  54.0 1.3 %collective-permute-done.1.other_ref = f32[768,128]{1,0:T(8,128)S(1)} collective-permute-done((f32[768,128]{1,0:T(8,128)S(1)}, f32[768,128]{1,0:T(8,128)S(1)}, u32[]{:S(2)}, u32[]{:S(2)}) %collective-permute-start.1) | collective-permute-done | bytes 393248 | tf_op jit(solution)/shard_map/ppermute | solution.py:242
  55.4 4.3 %shard_map.67 = f32[768,128]{1,0:T(8,128)S(1)} custom-call(s32[8,4,24]{2,1,0:T(4,128)S(1)} %bitcast.13, s32[8,4,24]{2,1,0:T(4,128)S(1)} %bitcast.16, bf16[7,8,128,128]{3,2,1,0:T(8,128)(2,1)S(1)} %get-tuple-element.18.weights, f32[768,128]{1,0:T(8,128)S(1)} %get-tuple-element.20.own_ref, f32[768,128]{1,0:T(8,128)S(1)} %collective-permute-done.1.other_ref), custom_call_target="tpu_custom_call" | custom-call | tf_op jit(solution)/shard_map/pallas_call | solution.py:280
  59.6 20.7 %all_to_all.11 = f32[64,1,1536]{2,1,0:T(1,128)S(1)} all-to-all(f32[64,1,1536]{2,1,0:T(1,128)S(1)} %bitcast.7), channel_id=1, replica_groups=mesh['z1'=2,'z0'=2,'y1'=2,'y0'=2,'x1'=2,'x0'=2,'zh'=2,'c'=2] {'z1','z0',..., dimensions={0} | all-to-all | bytes 786432 | tf_op jit(solution)/shard_map/all_to_all | solution.py:238
  80.3 1.7 %shard_map.68 = f32[64,3072]{1,0:T(8,128)} custom-call(f32[768,128]{1,0:T(8,128)S(1)} %bitcast.9, bf16[24,256,128]{2,1,0:T(8,128)(2,1)S(1)} %get-tuple-element.22.weights), custom_call_target="tpu_custom_call" | custom-call | tf_op jit(solution)/shard_map/pallas_call | solution.py:283
  (1 shorter events, 0.0 us)
Async XLA Ops:
  0.0 7.8 %copy-start = (f32[8,8,64,64]{3,2,1,0:T(8,128)S(1)}, f32[8,8,64,64]{3,2,1,0:T(8,128)}, u32[]{:S(2)}) copy-start(f32[8,8,64,64]{3,2,1,0:T(8,128)} %tables.3) | copy-start | bytes 3145732
  0.0 7.8 %copy-start.1 = (f32[24,128,64]{1,2,0:T(8,128)S(1)}, f32[24,128,64]{1,2,0:T(8,128)}, u32[]{:S(2)}) copy-start(f32[24,128,64]{1,2,0:T(8,128)} %param.8) | copy-start | bytes 2359300
  5.6 10.2 %copy-start.4 = (f32[768,128]{1,0:T(8,128)S(1)}, f32[768,128]{1,0:T(8,128)}, u32[]{:S(2)}) copy-start(f32[768,128]{1,0:T(8,128)} %get-tuple-element.14) | copy-start | bytes 1179652
  5.6 10.2 %collective-permute-start = (f32[768,128]{1,0:T(8,128)}, f32[768,128]{1,0:T(8,128)S(1)}, u32[]{:S(2)}, u32[]{:S(2)}) collective-permute-start(f32[768,128]{1,0:T(8,128)} %get-tuple-element.15), channel_id=1, source_target_pairs={{0,16},{16,0},{1,17},{17,1},{2,18},{18,2},{3,19},{19,3},{4,20},{20... | collective-permute-start | bytes 1179656 | tf_op jit(solution)/shard_map/ppermute | solution.py:242
  7.8 37.3 %copy-start.2 = (s32[8,24,4]{1,2,0:T(4,128)S(1)}, s32[8,24,4]{1,2,0:T(4,128)}, u32[]{:S(2)}) copy-start(s32[8,24,4]{1,2,0:T(4,128)} %param.10) | copy-start | bytes 9220
  7.8 37.3 %copy-start.3 = (s32[8,24,4]{1,2,0:T(4,128)S(1)}, s32[8,24,4]{1,2,0:T(4,128)}, u32[]{:S(2)}) copy-start(s32[8,24,4]{1,2,0:T(4,128)} %param.11) | copy-start | bytes 9220
  50.5 4.8 %collective-permute-start.1 = (f32[768,128]{1,0:T(8,128)S(1)}, f32[768,128]{1,0:T(8,128)S(1)}, u32[]{:S(2)}, u32[]{:S(2)}) collective-permute-start(f32[768,128]{1,0:T(8,128)S(1)} %get-tuple-element.21), channel_id=1, source_target_pairs={{0,1},{1,0},{2,3},{3,2},{4,5},{5,4},{6,7},{7,6},{8,9},{9,8},{10,11... | collective-permute-start | bytes 1179656 | tf_op jit(solution)/shard_map/ppermute | solution.py:242
where the time goes:
time: 82.3 us; the launch traced here: 82 us
  blocking collectives  50 us (61%)
  Pallas kernels  18.6 us (23%)
  waiting for transfers between devices  7.68 us (9%)
  starting transfers between devices  5.7 us (7%)
    all_to_all x2, blocking collectives, exchange(): return lax.all_to_all(x, GROUP, 0, 0, tiled=True).reshape(rows, LANES)  50 us
    ppermute x2, waiting for transfers between devices, partner(): return lax.ppermute(x, axis, [(0, 1), (1, 0)])  7.68 us
    ppermute x2, starting transfers between devices, partner(): return lax.ppermute(x, axis, [(0, 1), (1, 0)])  5.7 us
    pallas_call x1, Pallas kernels, local(): call(start_kernel, [flat, flat], [SMEM, SMEM, HBM, HBM, HBM], [held, pltp...  5.57 us
    pallas_call x1, Pallas kernels, local(): call(middle_kernel, [flat, flat], [SMEM, SMEM, VMEM, VMEM], [held, held])  5.37 us
    pallas_call x1, Pallas kernels, local(): call(end_kernel, [flat], [SMEM, SMEM, VMEM, VMEM, VMEM], [held, held])  4.27 us
    pallas_call x1, Pallas kernels, local(): call(root_kernel, [jax.ShapeDtypeStruct((waves, blocks * width), F32)], [...  1.72 us
  transfers between devices with their start and end apart: 2, of which 2 were waited for; matrix products, arithmetic and copies ran while one was open for 0% of the time, Pallas kernels for 2%

commit v1 on v0

--- a/solution.py
+++ b/solution.py
@@ -9,6 +9,7 @@
 
 BITS = ("z1", "z0", "y1", "y0", "x1", "x0", "zh", "c")
 GROUP = ("z1", "z0", "y1", "x1", "x0", "zh")
+FOLDED = "y0"
 FLIPS = ("y0", "y1", "z0", "z1", "c", "zh", "x0", "x1")
 LANES = 128
 F32, BF16 = jnp.float32, jnp.bfloat16
@@ -53,8 +54,8 @@
     return jnp.concatenate(groups, axis=0)
 
 
-def pair_rows(ref, pair):
-    return pl.ds(pair, ref.shape[0] // 12, stride=12)
+def pair_rows(ref, pair, first=0):
+    return pl.ds(first * 12 + pair, 64, stride=12)
 
 
 def put_pair(held, pair, x):
@@ -123,6 +124,15 @@
     return emit
 
 
+def give_by_bit(mine, out_ref):
+    def emit(pair, own_even, other_even, own_odd, other_odd):
+        own, other = join(own_even, own_odd), join(other_even, other_odd)
+        out_ref[pair_rows(out_ref, pair), :] = jnp.where(mine == 0, own, other)
+        out_ref[pair_rows(out_ref, pair, 64), :] = jnp.where(mine == 0, other, own)
+
+    return emit
+
+
 def run_levels(first, count, sources, types, held, weights, last):
     for i in range(count):
         now, then = held[i % 2], held[(i + 1) % 2]
@@ -131,7 +141,7 @@
 
 
 def start_kernel(
-    sources, types, tables, signals, maps, own_ref, other_ref, held, weights, table_in, signals_in, maps_in, sems
+    sources, types, mine, tables, signals, maps, out_ref, held, weights, table_in, signals_in, maps_in, sems
 ):
     blocks, rank, width = maps.shape
     parts = sems.shape[1]
@@ -166,7 +176,7 @@
         for copy in copies[i]:
             copy.wait()
         lax.fori_loop(i * some, (i + 1) * some, leaf, 0, unroll=some)
-    level_step(0, sources, types, held, weights, give_both(own_ref, other_ref))
+    level_step(0, sources, types, held, weights, give_by_bit(mine[0], out_ref))
 
 
 def prepare_kernel(tables, maps, weights, root_weights):
@@ -187,7 +197,7 @@
 
 def middle_kernel(sources, types, weights, x_ref, own_ref, other_ref, held, held_too):
     for pair in range(held.shape[0] // 2):
-        put_pair(held, pair, x_ref[pair_rows(x_ref, pair), :])
+        put_pair(held, pair, x_ref[pair_rows(x_ref, pair), :] + x_ref[pair_rows(x_ref, pair, 64), :])
     run_levels(1, 4, sources, types, (held, held_too), weights, give_both(own_ref, other_ref))
 
 
@@ -232,14 +242,26 @@
     )
 
 
-def exchange(x):
+def bit(name):
+    return 1 << (len(BITS) - 1 - BITS.index(name))
+
+
+def members(order):
+    rest = [bit(name) for name in BITS if name not in order]
+    bases = [sum(w for k, w in enumerate(rest) if i >> k & 1) for i in range(1 << len(rest))]
+    weight = [bit(name) for name in reversed(order)]
+    places = [sum(w for k, w in enumerate(weight) if i >> k & 1) for i in range(1 << len(order))]
+    return [[base + place for place in places] for base in bases]
+
+
+def exchange(x, order):
     rows = x.shape[0]
-    x = x.reshape(64, 1, rows * LANES // 64)
-    return lax.all_to_all(x, GROUP, 0, 0, tiled=True).reshape(rows, LANES)
-
-
-def partner(x, axis):
-    return lax.ppermute(x, axis, [(0, 1), (1, 0)])
+    x = x.reshape(1 << len(order), 1, (rows * LANES) >> len(order))
+    return lax.all_to_all(x, "d", 0, 0, tiled=True, axis_index_groups=members(order)).reshape(rows, LANES)
+
+
+def partner(x, name):
+    return lax.ppermute(x, "d", [(i, i ^ bit(name)) for i in range(1 << len(BITS))])
 
 
 def local(signals, leaf_maps, root_maps, translations, source_list, type_list):
@@ -250,10 +272,11 @@
     root_maps = jnp.swapaxes(root_maps, 1, 2)
     held = pltpu.VMEM((blocks, waves, LANES), BF16)
     flat = jax.ShapeDtypeStruct((waves * blocks // 2, LANES), F32)
-    own, other = call(
+    mine = (lax.axis_index("d") & bit(FOLDED)).reshape(1)
+    (x,) = call(
         start_kernel,
-        [flat, flat],
-        [SMEM, SMEM, HBM, HBM, HBM],
+        [jax.ShapeDtypeStruct((waves * blocks, LANES), F32)],
+        [SMEM, SMEM, SMEM, HBM, HBM, HBM],
         [
             held,
             pltpu.VMEM((kinds, 2 * rank, LANES), BF16),
@@ -263,8 +286,7 @@
             pltpu.SemaphoreType.DMA((3, 3)),
         ],
         mib=60,
-    )(sources, types, translations, signals, leaf_maps)
-    received = partner(other, "y0")
+    )(sources, types, mine, translations, signals, leaf_maps)
     weights, root_weights = call(
         prepare_kernel,
         [
@@ -274,19 +296,18 @@
         [VMEM, VMEM],
         cost=pl.CostEstimate(flops=2**24, bytes_accessed=2**23, transcendentals=0),
     )(translations, root_maps)
-    x, weights, root_weights = lax.optimization_barrier((own + received, weights, root_weights))
-    x = exchange(x)
+    x = exchange(x, (FOLDED,) + GROUP)
     own, other = call(middle_kernel, [flat, flat], [SMEM, SMEM, VMEM, VMEM], [held, held])(sources, types, weights, x)
     (x,) = call(end_kernel, [flat], [SMEM, SMEM, VMEM, VMEM, VMEM], [held, held])(
         sources, types, weights, own, partner(other, "c")
     )
     (out,) = call(root_kernel, [jax.ShapeDtypeStruct((waves, blocks * width), F32)], [VMEM, VMEM])(
-        exchange(x), root_weights
+        exchange(x, GROUP), root_weights
     )
     return out
 
 
 def solution(mesh):
-    fine = Mesh(mesh.devices.reshape((2,) * len(BITS)), BITS)
-    placed = (P(None, BITS), P(BITS, None, None), P(BITS, None, None), P(), P(), P())
-    return jax.shard_map(local, mesh=fine, in_specs=placed, out_specs=P(None, BITS), check_vma=False)
+    line = Mesh(mesh.devices.reshape(-1), ("d",))
+    placed = (P(None, "d"), P("d", None, None), P("d", None, None), P(), P(), P())
+    return jax.shard_map(local, mesh=line, in_specs=placed, out_specs=P(None, "d"), check_vma=False)

time: 82.3 us -> 83.3 us (1.012)
  blocking collectives: 50 us -> 22.3 us
  starting transfers between devices: 5.7 us -> 19.7 us
  waiting for transfers between devices: 7.68 us -> 17.3 us
  local copies, waits for them, and re-layouts: 0.02 us -> 5.03 us
    all_to_all x2 -> x1, blocking collectives: 50 us -> 22.3 us  [exchange(): lax.all_to_all(x, 'd', 0, 0, tiled=True, axis_index_groups=members(order))]
    all_to_all x0 -> x1, starting transfers between devices: none -> 16.3 us  [exchange(): lax.all_to_all(x, 'd', 0, 0, tiled=True, axis_index_groups=members(order))]
    all_to_all x0 -> x1, waiting for transfers between devices: none -> 15.9 us  [exchange(): lax.all_to_all(x, 'd', 0, 0, tiled=True, axis_index_groups=members(order))]
    ppermute x2 -> x1, waiting for transfers between devices: 7.68 us -> 1.35 us  [partner(): lax.ppermute(x, 'd', [(i, i ^ bit(name)) for i in range(1 << len(BITS))])]
    unnamed x10 -> x16, local copies, waits for them, and re-layouts: 0.02 us -> 5.03 us
    ppermute x2 -> x1, starting transfers between devices: 5.7 us -> 3.36 us  [partner(): lax.ppermute(x, 'd', [(i, i ^ bit(name)) for i in range(1 << len(BITS))])]
where the time goes in v1:
time: 83.3 us; the launch traced here: 83 us
  blocking collectives  22.3 us (27%)
  starting transfers between devices  19.7 us (24%)
  Pallas kernels  18.6 us (22%)
  waiting for transfers between devices  17.3 us (21%)
  local copies, waits for them, and re-layouts  5.03 us (6%)
    all_to_all x1, blocking collectives, exchange(): lax.all_to_all(x, 'd', 0, 0, tiled=True, axis_index_groups=members(order))  22.3 us
    all_to_all x1, starting transfers between devices, exchange(): lax.all_to_all(x, 'd', 0, 0, tiled=True, axis_index_groups=members(order))  16.3 us
    all_to_all x1, waiting for transfers between devices, exchange(): lax.all_to_all(x, 'd', 0, 0, tiled=True, axis_index_groups=members(order))  15.9 us
    pallas_call x1, Pallas kernels, local(): call(start_kernel, [jax.ShapeDtypeStruct((waves * blocks, LANES), F32)],...  5.6 us
    pallas_call x1, Pallas kernels, local(): call(middle_kernel, [flat, flat], [SMEM, SMEM, VMEM, VMEM], [held, held])  5.37 us
    unnamed x16, local copies, waits for them, and re-layouts  5.03 us
    pallas_call x1, Pallas kernels, local(): call(end_kernel, [flat], [SMEM, SMEM, VMEM, VMEM, VMEM], [held, held])  4.28 us
    ppermute x1, starting transfers between devices, partner(): lax.ppermute(x, 'd', [(i, i ^ bit(name)) for i in range(1 << len(BITS))])  3.36 us
  transfers between devices with their start and end apart: 2, of which 2 were waited for; matrix products, arithmetic and copies ran while one was open for 0% of the time, Pallas kernels for 2%

profile of v1, /device:TPU:1, one launch (start us, length us, event | category | flops | bytes accessed | tf_op | source)
XLA Modules:
  0.0 83.0 jit_solution(6786938499590114044)
XLA Ops:
  0.0 0.0 copy-start
  0.0 5.6 %shard_map.65 = f32[1536,128]{1,0:T(8,128)} custom-call(s32[8,4,24]{2,1,0:T(4,128)} %bitcast.12, s32[8,4,24]{2,1,0:T(4,128)} %bitcast.15, s32[1]{0:T(128)} %bitcast.3.mine, f32[8,8,64,64]{3,2,1,0:T(8,128)} %tables.3, f32[64,3072]{1,0:T(8,128)} %signals.1, f32[24,64,128]{2,1,0:T(8,128)} %maps.1), custom_call_target="tpu_custom_call" | custom-call | tf_op jit(solution)/shard_map/pallas_call | solution.py:276
  5.6 16.3 %all-to-all-start = ((f32[128,1,1536]{2,1,0:T(1,128)}), f32[128,1,1536]{2,1,0:T(1,128)S(1)}, u32[]{:S(2)}, u32[]{:S(2)}) async-start(f32[128,1,1536]{2,1,0:T(1,128)} %bitcast.18), calls=%async_computation | async-start | bytes 1572864 | tf_op jit(solution)/shard_map/all_to_all | solution.py:260
  22.0 0.0 copy-done
  22.0 0.0 copy-start.5
  22.0 1.1 %copy-done.5 = f32[24,128,64]{1,2,0:T(8,128)S(1)} copy-done((f32[24,128,64]{1,2,0:T(8,128)S(1)}, f32[24,128,64]{1,2,0:T(8,128)}, u32[]{:S(2)}) %copy-start.5) | copy-done | bytes 786456
  23.1 0.0 copy-start.6
  23.1 0.0 copy-start.7
  23.1 1.6 %shard_map.64 = (bf16[7,8,128,128]{3,2,1,0:T(8,128)(2,1)S(1)}, bf16[24,256,128]{2,1,0:T(8,128)(2,1)S(1)}) custom-call(f32[8,8,64,64]{3,2,1,0:T(8,128)S(1)} %copy-done, f32[24,64,128]{2,1,0:T(8,128)S(1)} %bitcast.11), custom_call_target="tpu_custom_call" | custom-call | flops 16777216 | bytes 8388608 | tf_op jit(solution)/shard_map/pallas_call | solution.py:290
  24.7 0.0 copy-start.1
  24.8 1.2 %copy-done.1 = bf16[7,8,128,128]{3,2,1,0:T(8,128)(2,1)} copy-done((bf16[7,8,128,128]{3,2,1,0:T(8,128)(2,1)}, bf16[7,8,128,128]{3,2,1,0:T(8,128)(2,1)S(1)}, u32[]{:S(2)}) %copy-start.1) | copy-done | bytes 1835032
  26.0 0.0 copy-start.3
  26.0 1.1 %copy-done.3 = bf16[24,256,128]{2,1,0:T(8,128)(2,1)} copy-done((bf16[24,256,128]{2,1,0:T(8,128)(2,1)}, bf16[24,256,128]{2,1,0:T(8,128)(2,1)S(1)}, u32[]{:S(2)}) %copy-start.3) | copy-done | bytes 1572888
  27.1 15.9 %all-to-all-done = f32[128,1,1536]{2,1,0:T(1,128)S(1)} async-done(((f32[128,1,1536]{2,1,0:T(1,128)}), f32[128,1,1536]{2,1,0:T(1,128)S(1)}, u32[]{:S(2)}, u32[]{:S(2)}) %all-to-all-start) | async-done | bytes 786464 | tf_op jit(solution)/shard_map/all_to_all | solution.py:260
  43.1 0.0 copy-done.6
  43.1 0.0 copy-done.7
  43.1 0.0 copy-start.2
  43.1 1.5 %copy-done.2 = bf16[7,8,128,128]{3,2,1,0:T(8,128)(2,1)S(1)} copy-done((bf16[7,8,128,128]{3,2,1,0:T(8,128)(2,1)S(1)}, bf16[7,8,128,128]{3,2,1,0:T(8,128)(2,1)}, u32[]{:S(2)}) %copy-start.2) | copy-done | bytes 1835032
  44.6 5.4 %shard_map.66 = (f32[768,128]{1,0:T(8,128)S(1)}, f32[768,128]{1,0:T(8,128)S(1)}) custom-call(s32[8,4,24]{2,1,0:T(4,128)S(1)} %bitcast.13, s32[8,4,24]{2,1,0:T(4,128)S(1)} %bitcast.16, bf16[7,8,128,128]{3,2,1,0:T(8,128)(2,1)S(1)} %copy-done.2, f32[1536,128]{1,0:T(8,128)S(1)} %bitcast.8), custom_call_target="tpu_custom_call" | custom-call | tf_op jit(solution)/shard_map/pallas_call | solution.py:300
  50.0 3.4 %collective-permute-start = (f32[768,128]{1,0:T(8,128)S(1)}, f32[768,128]{1,0:T(8,128)S(1)}, u32[]{:S(2)}, u32[]{:S(2)}) collective-permute-start(f32[768,128]{1,0:T(8,128)S(1)} %get-tuple-element.11), channel_id=1, source_target_pairs={{0,1},{1,0},{2,3},{3,2},{4,5},{5,4},{6,7},{7,6},{8,9},{9,8},{10,11... | collective-permute-start | bytes 1179656 | tf_op jit(solution)/shard_map/ppermute | solution.py:264
  53.3 1.3 %collective-permute-done.other_ref = f32[768,128]{1,0:T(8,128)S(1)} collective-permute-done((f32[768,128]{1,0:T(8,128)S(1)}, f32[768,128]{1,0:T(8,128)S(1)}, u32[]{:S(2)}, u32[]{:S(2)}) %collective-permute-start) | collective-permute-done | bytes 393248 | tf_op jit(solution)/shard_map/ppermute | solution.py:264
  54.7 0.0 copy-start.4
  54.7 4.3 %shard_map.67 = f32[768,128]{1,0:T(8,128)S(1)} custom-call(s32[8,4,24]{2,1,0:T(4,128)S(1)} %bitcast.14, s32[8,4,24]{2,1,0:T(4,128)S(1)} %bitcast.17, bf16[7,8,128,128]{3,2,1,0:T(8,128)(2,1)S(1)} %copy-done.2, f32[768,128]{1,0:T(8,128)S(1)} %get-tuple-element.10.own_ref, f32[768,128]{1,0:T(8,128)S(1)} %collective-permute-done.other_ref), custom_call_target="tpu_custom_call" | custom-call | tf_op jit(solution)/shard_map/pallas_call | solution.py:301
  59.0 22.3 %all_to_all.10 = f32[64,1,1536]{2,1,0:T(1,128)S(1)} all-to-all(f32[64,1,1536]{2,1,0:T(1,128)S(1)} %bitcast.9), channel_id=1, replica_groups={{0,2,4,6,8,10,12,14,32,34,36,38,40,42,44,46,64,66,68,70,72,74,76,78,96,..., dimensions={0} | all-to-all | bytes 786432 | tf_op jit(solution)/shard_map/all_to_all | solution.py:260
  81.3 0.0 copy-done.4
  81.3 1.7 %shard_map.68 = f32[64,3072]{1,0:T(8,128)} custom-call(f32[768,128]{1,0:T(8,128)S(1)} %bitcast.10, bf16[24,256,128]{2,1,0:T(8,128)(2,1)S(1)} %copy-done.4), custom_call_target="tpu_custom_call" | custom-call | tf_op jit(solution)/shard_map/pallas_call | solution.py:304
Async XLA Ops:
  0.0 22.0 %copy-start = (f32[8,8,64,64]{3,2,1,0:T(8,128)S(1)}, f32[8,8,64,64]{3,2,1,0:T(8,128)}, u32[]{:S(2)}) copy-start(f32[8,8,64,64]{3,2,1,0:T(8,128)} %tables.3) | copy-start | bytes 3145732
  5.6 37.5 %all-to-all-start = ((f32[128,1,1536]{2,1,0:T(1,128)}), f32[128,1,1536]{2,1,0:T(1,128)S(1)}, u32[]{:S(2)}, u32[]{:S(2)}) async-start(f32[128,1,1536]{2,1,0:T(1,128)} %bitcast.18), calls=%async_computation | async-start | bytes 1572864 | tf_op jit(solution)/shard_map/all_to_all | solution.py:260
  22.0 1.1 %copy-start.5 = (f32[24,128,64]{1,2,0:T(8,128)S(1)}, f32[24,128,64]{1,2,0:T(8,128)}, u32[]{:S(2)}) copy-start(f32[24,128,64]{1,2,0:T(8,128)} %param.8) | copy-start | bytes 2359300
  23.1 20.0 %copy-start.6 = (s32[8,24,4]{1,2,0:T(4,128)S(1)}, s32[8,24,4]{1,2,0:T(4,128)}, u32[]{:S(2)}) copy-start(s32[8,24,4]{1,2,0:T(4,128)} %param.10) | copy-start | bytes 9220
  23.1 20.0 %copy-start.7 = (s32[8,24,4]{1,2,0:T(4,128)S(1)}, s32[8,24,4]{1,2,0:T(4,128)}, u32[]{:S(2)}) copy-start(s32[8,24,4]{1,2,0:T(4,128)} %param.11) | copy-start | bytes 9220
  24.7 1.3 %copy-start.1 = (bf16[7,8,128,128]{3,2,1,0:T(8,128)(2,1)}, bf16[7,8,128,128]{3,2,1,0:T(8,128)(2,1)S(1)}, u32[]{:S(2)}) copy-start(bf16[7,8,128,128]{3,2,1,0:T(8,128)(2,1)S(1)} %get-tuple-element.9.weights) | copy-start | bytes 5505028
  26.0 1.1 %copy-start.3 = (bf16[24,256,128]{2,1,0:T(8,128)(2,1)}, bf16[24,256,128]{2,1,0:T(8,128)(2,1)S(1)}, u32[]{:S(2)}) copy-start(bf16[24,256,128]{2,1,0:T(8,128)(2,1)S(1)} %get-tuple-element.12.weights) | copy-start | bytes 4718596
  43.1 1.5 %copy-start.2 = (bf16[7,8,128,128]{3,2,1,0:T(8,128)(2,1)S(1)}, bf16[7,8,128,128]{3,2,1,0:T(8,128)(2,1)}, u32[]{:S(2)}) copy-start(bf16[7,8,128,128]{3,2,1,0:T(8,128)(2,1)} %copy-done.1) | copy-start | bytes 5505028
  50.0 4.7 %collective-permute-start = (f32[768,128]{1,0:T(8,128)S(1)}, f32[768,128]{1,0:T(8,128)S(1)}, u32[]{:S(2)}, u32[]{:S(2)}) collective-permute-start(f32[768,128]{1,0:T(8,128)S(1)} %get-tuple-element.11), channel_id=1, source_target_pairs={{0,1},{1,0},{2,3},{3,2},{4,5},{5,4},{6,7},{7,6},{8,9},{9,8},{10,11... | collective-permute-start | bytes 1179656 | tf_op jit(solution)/shard_map/ppermute | solution.py:264
  54.7 26.6 %copy-start.4 = (bf16[24,256,128]{2,1,0:T(8,128)(2,1)S(1)}, bf16[24,256,128]{2,1,0:T(8,128)(2,1)}, u32[]{:S(2)}) copy-start(bf16[24,256,128]{2,1,0:T(8,128)(2,1)} %copy-done.3) | copy-start | bytes 4718596

commit v2 on v1

--- a/solution.py
+++ b/solution.py
@@ -137,17 +137,19 @@
     for i in range(count):
         now, then = held[i % 2], held[(i + 1) % 2]
         emit = last if i == count - 1 else flip_and_keep(then, row_mask(first + i))
-        level_step(first + i, sources, types, now, weights.at[first + i - 1], emit)
+        level_step(first + i, sources, types, now, weights.at[i], emit)
 
 
 def start_kernel(
-    sources, types, mine, tables, signals, maps, out_ref, held, weights, table_in, signals_in, maps_in, sems
+    sources, types, mine, tables, signals, maps, out_ref, early, held, weights, table_in, signals_in, maps_in, sems, table_sems
 ):
     blocks, rank, width = maps.shape
     parts = sems.shape[1]
     some = blocks // parts
-    table_copy = pltpu.make_async_copy(tables.at[0], table_in, sems.at[2, 0])
-    table_copy.start()
+    table_copies = []
+    for level in range(table_in.shape[0]):
+        table_copies.append(pltpu.make_async_copy(tables.at[level], table_in.at[level], table_sems.at[level]))
+        table_copies[-1].start()
     copies = []
     for i in range(parts):
         lanes, rows = pl.ds(i * some * width, some * width), pl.ds(i * some, some)
@@ -159,9 +161,10 @@
         )
         for copy in copies[-1]:
             copy.start()
-    table_copy.wait()
-    for kind in range(weights.shape[0]):
-        put_weights(table_in[kind], weights.at[kind])
+    for level, copy in enumerate(table_copies):
+        copy.wait()
+        for kind in range(weights.shape[0]):
+            put_weights(table_in[level, kind], weights.at[kind] if level == 0 else early.at[level - 1, kind])
 
     def leaf(k, carry):
         wave_hi, wave_lo = split(signals_in[:, pl.ds(pl.multiple_of(k * width, width), width)])
@@ -179,13 +182,17 @@
     level_step(0, sources, types, held, weights, give_by_bit(mine[0], out_ref))
 
 
-def prepare_kernel(tables, maps, weights, root_weights):
+def prepare_tables(tables, weights):
     def table(level, carry):
         for kind in range(tables.shape[1]):
-            put_weights(tables[level + 1, kind], weights.at[level, kind])
-        return carry
-
-    lax.fori_loop(0, tables.shape[0] - 1, table, 0)
+            put_weights(tables[level, kind], weights.at[level, kind])
+        return carry
+
+    lax.fori_loop(0, tables.shape[0], table, 0)
+
+
+def prepare_late(tables, maps, weights, root_weights):
+    prepare_tables(tables.at[5:], weights)
 
     def root(block, carry):
         hi, lo = split(maps[block])
@@ -273,34 +280,35 @@
     held = pltpu.VMEM((blocks, waves, LANES), BF16)
     flat = jax.ShapeDtypeStruct((waves * blocks // 2, LANES), F32)
     mine = (lax.axis_index("d") & bit(FOLDED)).reshape(1)
-    (x,) = call(
+    def prepared(count):
+        return jax.ShapeDtypeStruct((count, kinds, 2 * rank, LANES), BF16)
+
+    x, early = call(
         start_kernel,
-        [jax.ShapeDtypeStruct((waves * blocks, LANES), F32)],
+        [jax.ShapeDtypeStruct((waves * blocks, LANES), F32), prepared(4)],
         [SMEM, SMEM, SMEM, HBM, HBM, HBM],
         [
             held,
             pltpu.VMEM((kinds, 2 * rank, LANES), BF16),
-            pltpu.VMEM((kinds, rank, rank), F32),
+            pltpu.VMEM((5, kinds, rank, rank), F32),
             pltpu.VMEM((waves, blocks * width), F32),
             pltpu.VMEM((blocks, rank, width), F32),
-            pltpu.SemaphoreType.DMA((3, 3)),
+            pltpu.SemaphoreType.DMA((2, 3)),
+            pltpu.SemaphoreType.DMA((5,)),
         ],
         mib=60,
     )(sources, types, mine, translations, signals, leaf_maps)
-    weights, root_weights = call(
-        prepare_kernel,
-        [
-            jax.ShapeDtypeStruct((levels - 1, kinds, 2 * rank, LANES), BF16),
-            jax.ShapeDtypeStruct((blocks, 4 * rank, width), BF16),
-        ],
+    x = exchange(x, (FOLDED,) + GROUP)
+    own, other = call(middle_kernel, [flat, flat], [SMEM, SMEM, VMEM, VMEM], [held, held])(sources, types, early, x)
+    other, translations, root_maps = lax.optimization_barrier((other, translations, root_maps))
+    received = partner(other, "c")
+    late, root_weights = call(
+        prepare_late,
+        [prepared(3), jax.ShapeDtypeStruct((blocks, 4 * rank, width), BF16)],
         [VMEM, VMEM],
-        cost=pl.CostEstimate(flops=2**24, bytes_accessed=2**23, transcendentals=0),
+        cost=pl.CostEstimate(flops=2**24, bytes_accessed=2**22, transcendentals=0),
     )(translations, root_maps)
-    x = exchange(x, (FOLDED,) + GROUP)
-    own, other = call(middle_kernel, [flat, flat], [SMEM, SMEM, VMEM, VMEM], [held, held])(sources, types, weights, x)
-    (x,) = call(end_kernel, [flat], [SMEM, SMEM, VMEM, VMEM, VMEM], [held, held])(
-        sources, types, weights, own, partner(other, "c")
-    )
+    (x,) = call(end_kernel, [flat], [SMEM, SMEM, VMEM, VMEM, VMEM], [held, held])(sources, types, late, own, received)
     (out,) = call(root_kernel, [jax.ShapeDtypeStruct((waves, blocks * width), F32)], [VMEM, VMEM])(
         exchange(x, GROUP), root_weights
     )

time: 83.3 us -> 84.2 us (1.011)
  blocking collectives: 22.3 us -> 59.9 us
  waiting for transfers between devices: 17.3 us -> 0.57 us
  starting transfers between devices: 19.7 us -> 3.37 us
  local copies, waits for them, and re-layouts: 5.03 us -> 1.24 us
    all_to_all x1 -> x2, blocking collectives: 22.3 us -> 59.9 us  [exchange(): lax.all_to_all(x, 'd', 0, 0, tiled=True, axis_index_groups=members(order))]
    all_to_all x1 -> x0, starting transfers between devices: 16.3 us -> none  [exchange(): lax.all_to_all(x, 'd', 0, 0, tiled=True, axis_index_groups=members(order))]
    all_to_all x1 -> x0, waiting for transfers between devices: 15.9 us -> none  [exchange(): lax.all_to_all(x, 'd', 0, 0, tiled=True, axis_index_groups=members(order))]
    unnamed x16 -> x10, local copies, waits for them, and re-layouts: 5.03 us -> 1.24 us
  transfers between devices with their start and end apart: 2 -> 1, of which waited for: 2 -> 1; matrix products, arithmetic and copies ran while one was open for 0% -> 0% of each run, Pallas kernels for 2% -> 1%
where the time goes in v2:
time: 84.2 us; the launch traced here: 83.9 us
  blocking collectives  59.9 us (71%)
  Pallas kernels  18.8 us (22%)
  starting transfers between devices  3.37 us (4%)
  local copies, waits for them, and re-layouts  1.24 us (1%)
    all_to_all x2, blocking collectives, exchange(): lax.all_to_all(x, 'd', 0, 0, tiled=True, axis_index_groups=members(order))  59.9 us
    pallas_call x1, Pallas kernels, local(): call(start_kernel, [jax.ShapeDtypeStruct((waves * blocks, LANES), F32), p...  6.7 us
    pallas_call x1, Pallas kernels, local(): call(middle_kernel, [flat, flat], [SMEM, SMEM, VMEM, VMEM], [held, held])  5.37 us
    pallas_call x1, Pallas kernels, local(): call(end_kernel, [flat], [SMEM, SMEM, VMEM, VMEM, VMEM], [held, held])  4.27 us
    ppermute x1, starting transfers between devices, partner(): lax.ppermute(x, 'd', [(i, i ^ bit(name)) for i in range(1 << len(BITS))])  3.37 us
    pallas_call x1, Pallas kernels, local(): call(root_kernel, [jax.ShapeDtypeStruct((waves, blocks * width), F32)], [...  1.71 us
  transfers between devices with their start and end apart: 1, of which 1 were waited for; matrix products, arithmetic and copies ran while one was open for 0% of the time, Pallas kernels for 1%

profile of v2, /device:TPU:1, one launch (start us, length us, event | category | flops | bytes accessed | tf_op | source)
XLA Modules:
  0.0 83.9 jit_solution(12241668690163968298)
XLA Ops:
  0.0 0.0 copy-start.3
  0.0 0.0 copy-start.4
  0.0 0.0 copy-start.2
  0.0 6.7 %shard_map.64 = (f32[1536,128]{1,0:T(8,128)}, bf16[4,8,128,128]{3,2,1,0:T(8,128)(2,1)}) custom-call(s32[8,4,24]{2,1,0:T(4,128)} %bitcast.12, s32[8,4,24]{2,1,0:T(4,128)} %bitcast.15, s32[1]{0:T(128)} %bitcast.2.mine, f32[8,8,64,64]{3,2,1,0:T(8,128)} %tables.2, f32[64,3072]{1,0:T(8,128)} %signals.1, f32[24,64,128]{2,1,0:T(8,128)} %maps.1), custom_call_target="tpu_custom_call" | custom-call | tf_op jit(solution)/shard_map/pallas_call | solution.py:286
  6.7 0.0 copy-start
  6.7 37.6 %all_to_all.10 = f32[128,1,1536]{2,1,0:T(1,128)S(1)} all-to-all(f32[128,1,1536]{2,1,0:T(1,128)} %bitcast.18), channel_id=1, replica_groups={{0,2,4,6,8,10,12,14,32,34,36,38,40,42,44,46,64,66,68,70,72,74,76,78,96,..., dimensions={0} | all-to-all | bytes 1572864 | tf_op jit(solution)/shard_map/all_to_all | solution.py:267
  44.3 0.0 copy-done.3
  44.3 0.0 copy-done.4
  44.3 0.0 copy-start.1
  44.3 1.2 %copy-done.1 = bf16[4,8,128,128]{3,2,1,0:T(8,128)(2,1)S(1)} copy-done((bf16[4,8,128,128]{3,2,1,0:T(8,128)(2,1)S(1)}, bf16[4,8,128,128]{3,2,1,0:T(8,128)(2,1)}, u32[]{:S(2)}) %copy-start.1) | copy-done | bytes 1048600
  45.5 5.4 %shard_map.65 = (f32[768,128]{1,0:T(8,128)S(1)}, f32[768,128]{1,0:T(8,128)S(1)}) custom-call(s32[8,4,24]{2,1,0:T(4,128)S(1)} %bitcast.13, s32[8,4,24]{2,1,0:T(4,128)S(1)} %bitcast.16, bf16[4,8,128,128]{3,2,1,0:T(8,128)(2,1)S(1)} %copy-done.1, f32[1536,128]{1,0:T(8,128)S(1)} %bitcast.8), custom_call_target="tpu_custom_call" | custom-call | tf_op jit(solution)/shard_map/pallas_call | solution.py:302
  50.9 3.4 %collective-permute-start = (f32[768,128]{1,0:T(8,128)S(1)}, f32[768,128]{1,0:T(8,128)S(1)}, u32[]{:S(2)}, u32[]{:S(2)}) collective-permute-start(f32[768,128]{1,0:T(8,128)S(1)} %get-tuple-element.21), channel_id=1, source_target_pairs={{0,1},{1,0},{2,3},{3,2},{4,5},{5,4},{6,7},{7,6},{8,9},{9,8},{10,11... | collective-permute-start | bytes 1179656 | tf_op jit(solution)/shard_map/ppermute | solution.py:271
  54.3 0.0 copy-done.2
  54.3 0.0 copy-done
  54.3 0.8 shard_map.66
  55.1 0.6 collective-permute-done.other_ref
  55.6 4.3 %shard_map.67 = f32[768,128]{1,0:T(8,128)S(1)} custom-call(s32[8,4,24]{2,1,0:T(4,128)S(1)} %bitcast.14, s32[8,4,24]{2,1,0:T(4,128)S(1)} %bitcast.17, bf16[3,8,128,128]{3,2,1,0:T(8,128)(2,1)S(1)} %get-tuple-element.19.weights, f32[768,128]{1,0:T(8,128)S(1)} %get-tuple-element.20.own_ref, f32[768,128]{1,0:T(8,128)S(1)} %collective-permute-done.other_ref), custom_call_target="tpu_custom_call" | custom-call | tf_op jit(solution)/shard_map/pallas_call | solution.py:311
  59.9 22.3 %all_to_all.11 = f32[64,1,1536]{2,1,0:T(1,128)S(1)} all-to-all(f32[64,1,1536]{2,1,0:T(1,128)S(1)} %bitcast.9), channel_id=1, replica_groups={{0,2,4,6,8,10,12,14,32,34,36,38,40,42,44,46,64,66,68,70,72,74,76,78,96,..., dimensions={0} | all-to-all | bytes 786432 | tf_op jit(solution)/shard_map/all_to_all | solution.py:267
  82.2 1.7 %shard_map.68 = f32[64,3072]{1,0:T(8,128)} custom-call(f32[768,128]{1,0:T(8,128)S(1)} %bitcast.10, bf16[24,256,128]{2,1,0:T(8,128)(2,1)S(1)} %get-tuple-element.22.weights), custom_call_target="tpu_custom_call" | custom-call | tf_op jit(solution)/shard_map/pallas_call | solution.py:312
Async XLA Ops:
  0.0 44.3 %copy-start.3 = (s32[8,24,4]{1,2,0:T(4,128)S(1)}, s32[8,24,4]{1,2,0:T(4,128)}, u32[]{:S(2)}) copy-start(s32[8,24,4]{1,2,0:T(4,128)} %param.10) | copy-start | bytes 9220
  0.0 44.3 %copy-start.4 = (s32[8,24,4]{1,2,0:T(4,128)S(1)}, s32[8,24,4]{1,2,0:T(4,128)}, u32[]{:S(2)}) copy-start(s32[8,24,4]{1,2,0:T(4,128)} %param.11) | copy-start | bytes 9220
  0.0 54.3 %copy-start.2 = (f32[24,128,64]{1,2,0:T(8,128)S(1)}, f32[24,128,64]{1,2,0:T(8,128)}, u32[]{:S(2)}) copy-start(f32[24,128,64]{1,2,0:T(8,128)} %param.8) | copy-start | bytes 2359300
  6.7 47.6 %copy-start = (f32[8,8,64,64]{3,2,1,0:T(8,128)S(1)}, f32[8,8,64,64]{3,2,1,0:T(8,128)}, u32[]{:S(2)}) copy-start(f32[8,8,64,64]{3,2,1,0:T(8,128)} %tables.2) | copy-start | bytes 3145732
  44.3 1.2 %copy-start.1 = (bf16[4,8,128,128]{3,2,1,0:T(8,128)(2,1)S(1)}, bf16[4,8,128,128]{3,2,1,0:T(8,128)(2,1)}, u32[]{:S(2)}) copy-start(bf16[4,8,128,128]{3,2,1,0:T(8,128)(2,1)} %get-tuple-element.14.weights) | copy-start | bytes 3145732
  50.9 4.7 %collective-permute-start = (f32[768,128]{1,0:T(8,128)S(1)}, f32[768,128]{1,0:T(8,128)S(1)}, u32[]{:S(2)}, u32[]{:S(2)}) collective-permute-start(f32[768,128]{1,0:T(8,128)S(1)} %get-tuple-element.21), channel_id=1, source_target_pairs={{0,1},{1,0},{2,3},{3,2},{4,5},{5,4},{6,7},{7,6},{8,9},{9,8},{10,11... | collective-permute-start | bytes 1179656 | tf_op jit(solution)/shard_map/ppermute | solution.py:271

commit v3 on v2

--- a/solution.py
+++ b/solution.py
@@ -245,7 +245,7 @@
         out_specs=[VMEM] * len(outs),
         scratch_shapes=scratch,
         cost_estimate=cost,
-        compiler_params=pltpu.CompilerParams(vmem_limit_bytes=mib * 2**20),
+        compiler_params=pltpu.CompilerParams(vmem_limit_bytes=int(mib * 2**20)),
     )
 
 
@@ -296,7 +296,7 @@
             pltpu.SemaphoreType.DMA((2, 3)),
             pltpu.SemaphoreType.DMA((5,)),
         ],
-        mib=60,
+        mib=53,
     )(sources, types, mine, translations, signals, leaf_maps)
     x = exchange(x, (FOLDED,) + GROUP)
     own, other = call(middle_kernel, [flat, flat], [SMEM, SMEM, VMEM, VMEM], [held, held])(sources, types, early, x)

time: 84.2 us -> 85.1 us (1.011)
  local copies, waits for them, and re-layouts: 1.24 us -> 2.67 us
    unnamed x10, local copies, waits for them, and re-layouts: 1.24 us -> 2.67 us
where the time goes in v3:
time: 85.1 us; the launch traced here: 84.8 us
  blocking collectives  59.7 us (70%)
  Pallas kernels  18.4 us (22%)
  starting transfers between devices  3.36 us (4%)
  local copies, waits for them, and re-layouts  2.67 us (3%)
    all_to_all x2, blocking collectives, exchange(): lax.all_to_all(x, 'd', 0, 0, tiled=True, axis_index_groups=members(order))  59.7 us
    pallas_call x1, Pallas kernels, local(): call(start_kernel, [jax.ShapeDtypeStruct((waves * blocks, LANES), F32), p...  6.32 us
    pallas_call x1, Pallas kernels, local(): call(middle_kernel, [flat, flat], [SMEM, SMEM, VMEM, VMEM], [held, held])  5.37 us
    pallas_call x1, Pallas kernels, local(): call(end_kernel, [flat], [SMEM, SMEM, VMEM, VMEM, VMEM], [held, held])  4.27 us
    ppermute x1, starting transfers between devices, partner(): lax.ppermute(x, 'd', [(i, i ^ bit(name)) for i in range(1 << len(BITS))])  3.36 us
    unnamed x10, local copies, waits for them, and re-layouts  2.67 us
    pallas_call x1, Pallas kernels, local(): call(root_kernel, [jax.ShapeDtypeStruct((waves, blocks * width), F32)], [...  1.71 us
  transfers between devices with their start and end apart: 1, of which 1 were waited for; matrix products, arithmetic and copies ran while one was open for 0% of the time, Pallas kernels for 1%

profile of v3, /device:TPU:1, one launch (start us, length us, event | category | flops | bytes accessed | tf_op | source)
XLA Modules:
  0.0 84.8 jit_solution(895829057237746392)
XLA Ops:
  0.0 0.0 copy-start.3
  0.0 0.7 copy-done.3
  0.7 0.0 copy-start.4
  0.7 0.7 copy-done.4
  1.4 0.0 copy-start.2
  1.4 6.3 %shard_map.64 = (f32[1536,128]{1,0:T(8,128)S(1)}, bf16[4,8,128,128]{3,2,1,0:T(8,128)(2,1)}) custom-call(s32[8,4,24]{2,1,0:T(4,128)S(1)} %bitcast.13, s32[8,4,24]{2,1,0:T(4,128)S(1)} %bitcast.16, s32[1]{0:T(128)} %bitcast.2.mine, f32[8,8,64,64]{3,2,1,0:T(8,128)} %tables.2, f32[64,3072]{1,0:T(8,128)} %signals.1, f32[24,64,128]{2,1,0:T(8,128)} %maps.1), custom_call_target="tpu_custom_call" | custom-call | tf_op jit(solution)/shard_map/pallas_call | solution.py:286
  7.8 0.0 copy-start
  7.8 37.4 %all_to_all.10 = f32[128,1,1536]{2,1,0:T(1,128)S(1)} all-to-all(f32[128,1,1536]{2,1,0:T(1,128)S(1)} %bitcast.11), channel_id=1, replica_groups={{0,2,4,6,8,10,12,14,32,34,36,38,40,42,44,46,64,66,68,70,72,74,76,78,96,..., dimensions={0} | all-to-all | bytes 1572864 | tf_op jit(solution)/shard_map/all_to_all | solution.py:267
  45.2 0.0 copy-start.1
  45.2 1.2 %copy-done.1 = bf16[4,8,128,128]{3,2,1,0:T(8,128)(2,1)S(1)} copy-done((bf16[4,8,128,128]{3,2,1,0:T(8,128)(2,1)S(1)}, bf16[4,8,128,128]{3,2,1,0:T(8,128)(2,1)}, u32[]{:S(2)}) %copy-start.1) | copy-done | bytes 1048600
  46.4 5.4 %shard_map.65 = (f32[768,128]{1,0:T(8,128)S(1)}, f32[768,128]{1,0:T(8,128)S(1)}) custom-call(s32[8,4,24]{2,1,0:T(4,128)S(1)} %bitcast.14, s32[8,4,24]{2,1,0:T(4,128)S(1)} %bitcast.17, bf16[4,8,128,128]{3,2,1,0:T(8,128)(2,1)S(1)} %copy-done.1, f32[1536,128]{1,0:T(8,128)S(1)} %bitcast.8), custom_call_target="tpu_custom_call" | custom-call | tf_op jit(solution)/shard_map/pallas_call | solution.py:302
  51.8 3.4 %collective-permute-start = (f32[768,128]{1,0:T(8,128)S(1)}, f32[768,128]{1,0:T(8,128)S(1)}, u32[]{:S(2)}, u32[]{:S(2)}) collective-permute-start(f32[768,128]{1,0:T(8,128)S(1)} %get-tuple-element.21), channel_id=1, source_target_pairs={{0,1},{1,0},{2,3},{3,2},{4,5},{5,4},{6,7},{7,6},{8,9},{9,8},{10,11... | collective-permute-start | bytes 1179656 | tf_op jit(solution)/shard_map/ppermute | solution.py:271
  55.1 0.0 copy-done.2
  55.1 0.0 copy-done
  55.1 0.8 shard_map.66
  55.9 0.6 collective-permute-done.other_ref
  56.5 4.3 %shard_map.67 = f32[768,128]{1,0:T(8,128)S(1)} custom-call(s32[8,4,24]{2,1,0:T(4,128)S(1)} %bitcast.15, s32[8,4,24]{2,1,0:T(4,128)S(1)} %bitcast.18, bf16[3,8,128,128]{3,2,1,0:T(8,128)(2,1)S(1)} %get-tuple-element.19.weights, f32[768,128]{1,0:T(8,128)S(1)} %get-tuple-element.20.own_ref, f32[768,128]{1,0:T(8,128)S(1)} %collective-permute-done.other_ref), custom_call_target="tpu_custom_call" | custom-call | tf_op jit(solution)/shard_map/pallas_call | solution.py:311
  60.7 22.3 %all_to_all.11 = f32[64,1,1536]{2,1,0:T(1,128)S(1)} all-to-all(f32[64,1,1536]{2,1,0:T(1,128)S(1)} %bitcast.9), channel_id=1, replica_groups={{0,2,4,6,8,10,12,14,32,34,36,38,40,42,44,46,64,66,68,70,72,74,76,78,96,..., dimensions={0} | all-to-all | bytes 786432 | tf_op jit(solution)/shard_map/all_to_all | solution.py:267
  83.1 1.7 %shard_map.68 = f32[64,3072]{1,0:T(8,128)} custom-call(f32[768,128]{1,0:T(8,128)S(1)} %bitcast.10, bf16[24,256,128]{2,1,0:T(8,128)(2,1)S(1)} %get-tuple-element.22.weights), custom_call_target="tpu_custom_call" | custom-call | tf_op jit(solution)/shard_map/pallas_call | solution.py:312
Async XLA Ops:
  0.0 0.7 copy-start.3
  0.7 0.7 copy-start.4
  1.4 53.7 %copy-start.2 = (f32[24,128,64]{1,2,0:T(8,128)S(1)}, f32[24,128,64]{1,2,0:T(8,128)}, u32[]{:S(2)}) copy-start(f32[24,128,64]{1,2,0:T(8,128)} %param.8) | copy-start | bytes 2359300
  7.8 47.4 %copy-start = (f32[8,8,64,64]{3,2,1,0:T(8,128)S(1)}, f32[8,8,64,64]{3,2,1,0:T(8,128)}, u32[]{:S(2)}) copy-start(f32[8,8,64,64]{3,2,1,0:T(8,128)} %tables.2) | copy-start | bytes 3145732
  45.2 1.2 %copy-start.1 = (bf16[4,8,128,128]{3,2,1,0:T(8,128)(2,1)S(1)}, bf16[4,8,128,128]{3,2,1,0:T(8,128)(2,1)}, u32[]{:S(2)}) copy-start(bf16[4,8,128,128]{3,2,1,0:T(8,128)(2,1)} %get-tuple-element.14.weights) | copy-start | bytes 3145732
  51.8 4.7 %collective-permute-start = (f32[768,128]{1,0:T(8,128)S(1)}, f32[768,128]{1,0:T(8,128)S(1)}, u32[]{:S(2)}, u32[]{:S(2)}) collective-permute-start(f32[768,128]{1,0:T(8,128)S(1)} %get-tuple-element.21), channel_id=1, source_target_pairs={{0,1},{1,0},{2,3},{3,2},{4,5},{5,4},{6,7},{7,6},{8,9},{9,8},{10,11... | collective-permute-start | bytes 1179656 | tf_op jit(solution)/shard_map/ppermute | solution.py:271

commit v4 on v0

--- a/solution.py
+++ b/solution.py
@@ -89,7 +89,17 @@
         emit(pair, *terms)
         return carry
 
-    lax.fori_loop(0, blocks // 2, pair_step, 0, unroll=6)
+    lax.fori_loop(0, blocks // 2, pair_step, 0, unroll=True)
+
+
+def half_level(level, entry, back, sources, types, held, weights, out_ref):
+    def pair_step(pair, carry):
+        even = two_terms(level, 2 * pair, entry, sources, types, back, held, weights)
+        odd = two_terms(level, 2 * pair + 1, entry, sources, types, back, held, weights)
+        out_ref[pair_rows(out_ref, pair), :] = join(even, odd)
+        return carry
+
+    lax.fori_loop(0, held.shape[0] // 2, pair_step, 0, unroll=True)
 
 
 def flip_and_keep(held, mask):
@@ -131,7 +141,7 @@
 
 
 def start_kernel(
-    sources, types, tables, signals, maps, own_ref, other_ref, held, weights, table_in, signals_in, maps_in, sems
+    sources, types, tables, signals, maps, other_ref, held, weights, table_in, signals_in, maps_in, sems
 ):
     blocks, rank, width = maps.shape
     parts = sems.shape[1]
@@ -166,10 +176,14 @@
         for copy in copies[i]:
             copy.wait()
         lax.fori_loop(i * some, (i + 1) * some, leaf, 0, unroll=some)
-    level_step(0, sources, types, held, weights, give_both(own_ref, other_ref))
-
-
-def prepare_kernel(tables, maps, weights, root_weights):
+    half_level(0, 2, blocks, sources, types, held, weights, other_ref)
+
+
+def prepare_kernel(sources, types, tables, maps, held, own_ref, weights, root_weights, weights_here):
+    for kind in range(tables.shape[1]):
+        put_weights(tables[0, kind], weights_here.at[kind])
+    half_level(0, 0, 0, sources, types, held, weights_here, own_ref)
+
     def table(level, carry):
         for kind in range(tables.shape[1]):
             put_weights(tables[level + 1, kind], weights.at[level, kind])
@@ -250,12 +264,11 @@
     root_maps = jnp.swapaxes(root_maps, 1, 2)
     held = pltpu.VMEM((blocks, waves, LANES), BF16)
     flat = jax.ShapeDtypeStruct((waves * blocks // 2, LANES), F32)
-    own, other = call(
+    other, left = call(
         start_kernel,
-        [flat, flat],
+        [flat, jax.ShapeDtypeStruct((blocks, waves, LANES), BF16)],
         [SMEM, SMEM, HBM, HBM, HBM],
         [
-            held,
             pltpu.VMEM((kinds, 2 * rank, LANES), BF16),
             pltpu.VMEM((kinds, rank, rank), F32),
             pltpu.VMEM((waves, blocks * width), F32),
@@ -265,15 +278,17 @@
         mib=60,
     )(sources, types, translations, signals, leaf_maps)
     received = partner(other, "y0")
-    weights, root_weights = call(
+    own, weights, root_weights = call(
         prepare_kernel,
         [
+            flat,
             jax.ShapeDtypeStruct((levels - 1, kinds, 2 * rank, LANES), BF16),
             jax.ShapeDtypeStruct((blocks, 4 * rank, width), BF16),
         ],
-        [VMEM, VMEM],
+        [SMEM, SMEM, VMEM, VMEM, VMEM],
+        [pltpu.VMEM((kinds, 2 * rank, LANES), BF16)],
         cost=pl.CostEstimate(flops=2**24, bytes_accessed=2**23, transcendentals=0),
-    )(translations, root_maps)
+    )(sources, types, translations, root_maps, left)
     x, weights, root_weights = lax.optimization_barrier((own + received, weights, root_weights))
     x = exchange(x)
     own, other = call(middle_kernel, [flat, flat], [SMEM, SMEM, VMEM, VMEM], [held, held])(sources, types, weights, x)

time: 82.3 us -> 80.1 us (0.973)
  waiting for transfers between devices: 7.68 us -> 4.89 us
  local copies, waits for them, and re-layouts: 0.02 us -> 1 us
    ppermute x2, waiting for transfers between devices: 7.68 us -> 4.89 us  [partner(): return lax.ppermute(x, axis, [(0, 1), (1, 0)])]
    pallas_call x2, Pallas kernels: 7.2 us -> 8.36 us  [the longest x1 4.93 us: local(): call(start_kernel, [flat, jax.ShapeDtypeStruct((blocks, waves, LANES), BF...]
    unnamed x10, local copies, waits for them, and re-layouts: 0.02 us -> 1 us
    pallas_call x1, Pallas kernels: 5.37 us -> 4.46 us  [local(): call(middle_kernel, [flat, flat], [SMEM, SMEM, VMEM, VMEM], [held, held])]
  transfers between devices with their start and end apart: 2 -> 2, of which waited for: 2 -> 2; matrix products, arithmetic and copies ran while one was open for 0% -> 0% of each run, Pallas kernels for 2% -> 4%
where the time goes in v4:
time: 80.1 us; the launch traced here: 79.9 us
  blocking collectives  50.1 us (63%)
  Pallas kernels  18.2 us (23%)
  starting transfers between devices  5.6 us (7%)
  waiting for transfers between devices  4.89 us (6%)
  local copies, waits for them, and re-layouts  1 us (1%)
    all_to_all x2, blocking collectives, exchange(): return lax.all_to_all(x, GROUP, 0, 0, tiled=True).reshape(rows, LANES)  50.1 us
    ppermute x2, starting transfers between devices, partner(): return lax.ppermute(x, axis, [(0, 1), (1, 0)])  5.6 us
    pallas_call x1, Pallas kernels, local(): call(start_kernel, [flat, jax.ShapeDtypeStruct((blocks, waves, LANES), BF...  4.93 us
    ppermute x2, waiting for transfers between devices, partner(): return lax.ppermute(x, axis, [(0, 1), (1, 0)])  4.89 us
    pallas_call x1, Pallas kernels, local(): call(middle_kernel, [flat, flat], [SMEM, SMEM, VMEM, VMEM], [held, held])  4.46 us
    pallas_call x1, Pallas kernels, local(): call(end_kernel, [flat], [SMEM, SMEM, VMEM, VMEM, VMEM], [held, held])  3.63 us
    pallas_call x1, Pallas kernels, local(): call(prepare_kernel, [flat, jax.ShapeDtypeStruct((levels - 1, kinds, 2 *...  3.43 us
    pallas_call x1, Pallas kernels, local(): call(root_kernel, [jax.ShapeDtypeStruct((waves, blocks * width), F32)], [...  1.71 us
  transfers between devices with their start and end apart: 2, of which 2 were waited for; matrix products, arithmetic and copies ran while one was open for 0% of the time, Pallas kernels for 4%

profile of v4, /device:TPU:1, one launch (start us, length us, event | category | flops | bytes accessed | tf_op | source)
XLA Modules:
  0.0 79.9 jit_solution(1803781513082917611)
XLA Ops:
  0.0 0.0 copy-start
  0.0 0.0 copy-start.1
  0.0 0.0 copy-start.3
  0.0 0.0 copy-start.4
  0.0 4.9 %shard_map.64 = (f32[768,128]{1,0:T(8,128)}, bf16[24,64,128]{2,1,0:T(8,128)(2,1)}) custom-call(s32[8,4,24]{2,1,0:T(4,128)} %bitcast.11, s32[8,4,24]{2,1,0:T(4,128)} %bitcast.15, f32[8,8,64,64]{3,2,1,0:T(8,128)} %tables.3, f32[64,3072]{1,0:T(8,128)} %signals.1, f32[24,64,128]{2,1,0:T(8,128)} %maps.1), custom_call_target="tpu_custom_call" | custom-call | tf_op jit(solution)/shard_map/pallas_call | solution.py:267
  5.0 2.2 %collective-permute-start = (f32[768,128]{1,0:T(8,128)}, f32[768,128]{1,0:T(8,128)S(1)}, u32[]{:S(2)}, u32[]{:S(2)}) collective-permute-start(f32[768,128]{1,0:T(8,128)} %get-tuple-element.17), channel_id=1, source_target_pairs={{0,16},{16,0},{1,17},{17,1},{2,18},{18,2},{3,19},{19,3},{4,20},{20... | collective-permute-start | bytes 1179656 | tf_op jit(solution)/shard_map/ppermute | solution.py:256
  7.2 0.0 copy-done
  7.2 0.0 copy-done.1
  7.2 0.0 copy-done.3
  7.2 0.0 copy-done.4
  7.2 0.0 copy-start.2
  7.2 1.0 %copy-done.2 = bf16[24,64,128]{2,1,0:T(8,128)(2,1)S(1)} copy-done((bf16[24,64,128]{2,1,0:T(8,128)(2,1)S(1)}, bf16[24,64,128]{2,1,0:T(8,128)(2,1)}, u32[]{:S(2)}) %copy-start.2) | copy-done | bytes 393240
  8.2 3.4 %shard_map.65 = (f32[768,128]{1,0:T(8,128)S(1)}, bf16[7,8,128,128]{3,2,1,0:T(8,128)(2,1)S(1)}, bf16[24,256,128]{2,1,0:T(8,128)(2,1)S(1)}) custom-call(s32[8,4,24]{2,1,0:T(4,128)S(1)} %bitcast.12, s32[8,4,24]{2,1,0:T(4,128)S(1)} %bitcast.16, f32[8,8,64,64]{3,2,1,0:T(8,128)S(1)} %copy-done, f32[24,64,128]{2,1,0:T(8,128)S(1)} %bitcast.10, ...), custom_call_target="tpu_custom_call" | custom-call | flops 16777216 | bytes 8388608 | tf_op jit(solution)/shard_map/pallas_call | solution.py:281
  11.6 3.5 %collective-permute-done = f32[768,128]{1,0:T(8,128)S(1)} collective-permute-done((f32[768,128]{1,0:T(8,128)}, f32[768,128]{1,0:T(8,128)S(1)}, u32[]{:S(2)}, u32[]{:S(2)}) %collective-permute-start) | collective-permute-done | bytes 393248 | tf_op jit(solution)/shard_map/ppermute | solution.py:256
  15.2 29.4 %all_to_all.10 = f32[64,1,1536]{2,1,0:T(1,128)S(1)} all-to-all(f32[64,1,1536]{2,1,0:T(1,128)S(1)} %bitcast.19), channel_id=1, replica_groups=mesh['z1'=2,'z0'=2,'y1'=2,'y0'=2,'x1'=2,'x0'=2,'zh'=2,'c'=2] {'z1','z0',..., dimensions={0} | all-to-all | bytes 786432 | tf_op jit(solution)/shard_map/all_to_all | solution.py:252
  44.6 4.5 %shard_map.66 = (f32[768,128]{1,0:T(8,128)S(1)}, f32[768,128]{1,0:T(8,128)S(1)}) custom-call(s32[8,4,24]{2,1,0:T(4,128)S(1)} %bitcast.13, s32[8,4,24]{2,1,0:T(4,128)S(1)} %bitcast.17, bf16[7,8,128,128]{3,2,1,0:T(8,128)(2,1)S(1)} %get-tuple-element.20.weights, f32[768,128]{1,0:T(8,128)S(1)} %bitcast.8), custom_call_target="tpu_custom_call" | custom-call | tf_op jit(solution)/shard_map/pallas_call | solution.py:294
  49.0 3.4 %collective-permute-start.1 = (f32[768,128]{1,0:T(8,128)S(1)}, f32[768,128]{1,0:T(8,128)S(1)}, u32[]{:S(2)}, u32[]{:S(2)}) collective-permute-start(f32[768,128]{1,0:T(8,128)S(1)} %get-tuple-element.23), channel_id=1, source_target_pairs={{0,1},{1,0},{2,3},{3,2},{4,5},{5,4},{6,7},{7,6},{8,9},{9,8},{10,11... | collective-permute-start | bytes 1179656 | tf_op jit(solution)/shard_map/ppermute | solution.py:256
  52.4 1.3 %collective-permute-done.1.other_ref = f32[768,128]{1,0:T(8,128)S(1)} collective-permute-done((f32[768,128]{1,0:T(8,128)S(1)}, f32[768,128]{1,0:T(8,128)S(1)}, u32[]{:S(2)}, u32[]{:S(2)}) %collective-permute-start.1) | collective-permute-done | bytes 393248 | tf_op jit(solution)/shard_map/ppermute | solution.py:256
  53.8 3.6 %shard_map.67 = f32[768,128]{1,0:T(8,128)S(1)} custom-call(s32[8,4,24]{2,1,0:T(4,128)S(1)} %bitcast.14, s32[8,4,24]{2,1,0:T(4,128)S(1)} %bitcast.18, bf16[7,8,128,128]{3,2,1,0:T(8,128)(2,1)S(1)} %get-tuple-element.20.weights, f32[768,128]{1,0:T(8,128)S(1)} %get-tuple-element.22.own_ref, f32[768,128]{1,0:T(8,128)S(1)} %collective-permute-done.1.other_ref), custom_call_target="tpu_custom_call" | custom-call | tf_op jit(solution)/shard_map/pallas_call | solution.py:295
  57.4 20.7 %all_to_all.11 = f32[64,1,1536]{2,1,0:T(1,128)S(1)} all-to-all(f32[64,1,1536]{2,1,0:T(1,128)S(1)} %bitcast.7), channel_id=1, replica_groups=mesh['z1'=2,'z0'=2,'y1'=2,'y0'=2,'x1'=2,'x0'=2,'zh'=2,'c'=2] {'z1','z0',..., dimensions={0} | all-to-all | bytes 786432 | tf_op jit(solution)/shard_map/all_to_all | solution.py:252
  78.1 1.7 %shard_map.68 = f32[64,3072]{1,0:T(8,128)} custom-call(f32[768,128]{1,0:T(8,128)S(1)} %bitcast.9, bf16[24,256,128]{2,1,0:T(8,128)(2,1)S(1)} %get-tuple-element.24.weights), custom_call_target="tpu_custom_call" | custom-call | tf_op jit(solution)/shard_map/pallas_call | solution.py:298
  (1 shorter events, 0.0 us)
Async XLA Ops:
  0.0 7.2 %copy-start = (f32[8,8,64,64]{3,2,1,0:T(8,128)S(1)}, f32[8,8,64,64]{3,2,1,0:T(8,128)}, u32[]{:S(2)}) copy-start(f32[8,8,64,64]{3,2,1,0:T(8,128)} %tables.3) | copy-start | bytes 3145732
  0.0 7.2 %copy-start.1 = (f32[24,128,64]{1,2,0:T(8,128)S(1)}, f32[24,128,64]{1,2,0:T(8,128)}, u32[]{:S(2)}) copy-start(f32[24,128,64]{1,2,0:T(8,128)} %param.8) | copy-start | bytes 2359300
  0.0 7.2 %copy-start.3 = (s32[8,24,4]{1,2,0:T(4,128)S(1)}, s32[8,24,4]{1,2,0:T(4,128)}, u32[]{:S(2)}) copy-start(s32[8,24,4]{1,2,0:T(4,128)} %param.10) | copy-start | bytes 9220
  0.0 7.2 %copy-start.4 = (s32[8,24,4]{1,2,0:T(4,128)S(1)}, s32[8,24,4]{1,2,0:T(4,128)}, u32[]{:S(2)}) copy-start(s32[8,24,4]{1,2,0:T(4,128)} %param.11) | copy-start | bytes 9220
  5.0 10.2 %collective-permute-start = (f32[768,128]{1,0:T(8,128)}, f32[768,128]{1,0:T(8,128)S(1)}, u32[]{:S(2)}, u32[]{:S(2)}) collective-permute-start(f32[768,128]{1,0:T(8,128)} %get-tuple-element.17), channel_id=1, source_target_pairs={{0,16},{16,0},{1,17},{17,1},{2,18},{18,2},{3,19},{19,3},{4,20},{20... | collective-permute-start | bytes 1179656 | tf_op jit(solution)/shard_map/ppermute | solution.py:256
  7.2 1.0 %copy-start.2 = (bf16[24,64,128]{2,1,0:T(8,128)(2,1)S(1)}, bf16[24,64,128]{2,1,0:T(8,128)(2,1)}, u32[]{:S(2)}) copy-start(bf16[24,64,128]{2,1,0:T(8,128)(2,1)} %get-tuple-element.15.held) | copy-start | bytes 1179652
  49.0 4.7 %collective-permute-start.1 = (f32[768,128]{1,0:T(8,128)S(1)}, f32[768,128]{1,0:T(8,128)S(1)}, u32[]{:S(2)}, u32[]{:S(2)}) collective-permute-start(f32[768,128]{1,0:T(8,128)S(1)} %get-tuple-element.23), channel_id=1, source_target_pairs={{0,1},{1,0},{2,3},{3,2},{4,5},{5,4},{6,7},{7,6},{8,9},{9,8},{10,11... | collective-permute-start | bytes 1179656 | tf_op jit(solution)/shard_map/ppermute | solution.py:256

commit v5 on v4

--- a/solution.py
+++ b/solution.py
@@ -137,11 +137,11 @@
     for i in range(count):
         now, then = held[i % 2], held[(i + 1) % 2]
         emit = last if i == count - 1 else flip_and_keep(then, row_mask(first + i))
-        level_step(first + i, sources, types, now, weights.at[first + i - 1], emit)
+        level_step(first + i, sources, types, now, weights.at[i], emit)
 
 
 def start_kernel(
-    sources, types, tables, signals, maps, other_ref, held, weights, table_in, signals_in, maps_in, sems
+    sources, types, tables, signals, maps, other_ref, left_ref, held, weights, table_in, signals_in, maps_in, sems
 ):
     blocks, rank, width = maps.shape
     parts = sems.shape[1]
@@ -176,20 +176,25 @@
         for copy in copies[i]:
             copy.wait()
         lax.fori_loop(i * some, (i + 1) * some, leaf, 0, unroll=some)
+    left_copy = pltpu.make_async_copy(held, left_ref, sems.at[2, 1])
+    left_copy.start()
     half_level(0, 2, blocks, sources, types, held, weights, other_ref)
-
-
-def prepare_kernel(sources, types, tables, maps, held, own_ref, weights, root_weights, weights_here):
+    left_copy.wait()
+
+
+def prepare_kernel(sources, types, tables, maps, held, own_ref, early, late, root_weights, weights_here):
     for kind in range(tables.shape[1]):
         put_weights(tables[0, kind], weights_here.at[kind])
     half_level(0, 0, 0, sources, types, held, weights_here, own_ref)
 
-    def table(level, carry):
-        for kind in range(tables.shape[1]):
-            put_weights(tables[level + 1, kind], weights.at[level, kind])
-        return carry
-
-    lax.fori_loop(0, tables.shape[0] - 1, table, 0)
+    for first, weights in ((1, early), (1 + early.shape[0], late)):
+
+        def table(level, carry, first=first, weights=weights):
+            for kind in range(tables.shape[1]):
+                put_weights(tables[first + level, kind], weights.at[level, kind])
+            return carry
+
+        lax.fori_loop(0, weights.shape[0], table, 0)
 
     def root(block, carry):
         hi, lo = split(maps[block])
@@ -199,10 +204,16 @@
     lax.fori_loop(0, maps.shape[0], root, 0, unroll=4)
 
 
-def middle_kernel(sources, types, weights, x_ref, own_ref, other_ref, held, held_too):
-    for pair in range(held.shape[0] // 2):
+def middle_kernel(sources, types, weights, x_ref, other_ref, left_ref, held, held_too):
+    blocks = held.shape[0]
+    for pair in range(blocks // 2):
         put_pair(held, pair, x_ref[pair_rows(x_ref, pair), :])
-    run_levels(1, 4, sources, types, (held, held_too), weights, give_both(own_ref, other_ref))
+    run_levels(1, 3, sources, types, (held, held_too), weights, flip_and_keep(left_ref, row_mask(3)))
+    half_level(4, 2, blocks, sources, types, left_ref, weights.at[3], other_ref)
+
+
+def own_kernel(sources, types, weights, left, own_ref):
+    half_level(4, 0, 0, sources, types, left, weights.at[0], own_ref)
 
 
 def end_kernel(sources, types, weights, own_ref, other_ref, out_ref, held, held_too):
@@ -214,18 +225,15 @@
 
 def root_kernel(x_ref, weights, out_ref):
     blocks, width = weights.shape[0], weights.shape[2]
-
-    def body(pair, carry):
-        x = x_ref[pair_rows(x_ref, pair), :]
+    first = pl.program_id(0) * (blocks // 2)
+    for pair in range(blocks // 2):
+        x = x_ref[pair_rows(x_ref, first + pair), :]
         turned = turn(x)
         low = low_lanes(x.shape)
         for block, value in ((2 * pair, jnp.where(low, x, turned)), (2 * pair + 1, jnp.where(low, turned, x))):
             left = hi_lo_lanes(value)
             out = jnp.dot(jnp.concatenate([left, left], axis=1), weights[block], preferred_element_type=F32)
-            out_ref[:, pl.ds(pl.multiple_of(block * width, width), width)] = out
-        return carry
-
-    lax.fori_loop(0, blocks // 2, body, 0, unroll=4)
+            out_ref[:, block * width : (block + 1) * width] = out
 
 
 VMEM = pl.BlockSpec(memory_space=pltpu.VMEM)
@@ -233,13 +241,13 @@
 HBM = pl.BlockSpec(memory_space=pltpu.HBM)
 
 
-def call(kernel, outs, specs, scratch=(), mib=12, cost=None):
+def call(kernel, outs, specs, scratch=(), mib=12, cost=None, out_specs=None, steps=1):
     return pl.pallas_call(
         kernel,
         out_shape=outs,
-        grid=(1,),
+        grid=(steps,),
         in_specs=specs,
-        out_specs=[VMEM] * len(outs),
+        out_specs=out_specs or [VMEM] * len(outs),
         scratch_shapes=scratch,
         cost_estimate=cost,
         compiler_params=pltpu.CompilerParams(vmem_limit_bytes=mib * 2**20),
@@ -269,6 +277,7 @@
         [flat, jax.ShapeDtypeStruct((blocks, waves, LANES), BF16)],
         [SMEM, SMEM, HBM, HBM, HBM],
         [
+            held,
             pltpu.VMEM((kinds, 2 * rank, LANES), BF16),
             pltpu.VMEM((kinds, rank, rank), F32),
             pltpu.VMEM((waves, blocks * width), F32),
@@ -276,28 +285,47 @@
             pltpu.SemaphoreType.DMA((3, 3)),
         ],
         mib=60,
+        out_specs=[VMEM, HBM],
     )(sources, types, translations, signals, leaf_maps)
     received = partner(other, "y0")
-    own, weights, root_weights = call(
+
+    def prepared(count):
+        return jax.ShapeDtypeStruct((count, kinds, 2 * rank, LANES), BF16)
+
+    own, early, late, root_weights = call(
         prepare_kernel,
-        [
-            flat,
-            jax.ShapeDtypeStruct((levels - 1, kinds, 2 * rank, LANES), BF16),
-            jax.ShapeDtypeStruct((blocks, 4 * rank, width), BF16),
-        ],
+        [flat, prepared(4), prepared(3), jax.ShapeDtypeStruct((blocks, 4 * rank, width), BF16)],
         [SMEM, SMEM, VMEM, VMEM, VMEM],
         [pltpu.VMEM((kinds, 2 * rank, LANES), BF16)],
         cost=pl.CostEstimate(flops=2**24, bytes_accessed=2**23, transcendentals=0),
     )(sources, types, translations, root_maps, left)
-    x, weights, root_weights = lax.optimization_barrier((own + received, weights, root_weights))
+    x, early, late, root_weights = lax.optimization_barrier((own + received, early, late, root_weights))
     x = exchange(x)
-    own, other = call(middle_kernel, [flat, flat], [SMEM, SMEM, VMEM, VMEM], [held, held])(sources, types, weights, x)
-    (x,) = call(end_kernel, [flat], [SMEM, SMEM, VMEM, VMEM, VMEM], [held, held])(
-        sources, types, weights, own, partner(other, "c")
-    )
-    (out,) = call(root_kernel, [jax.ShapeDtypeStruct((waves, blocks * width), F32)], [VMEM, VMEM])(
-        exchange(x), root_weights
-    )
+    other, left = call(
+        middle_kernel,
+        [flat, jax.ShapeDtypeStruct((blocks, waves, LANES), BF16)],
+        [SMEM, SMEM, VMEM, VMEM],
+        [held, held],
+    )(sources, types, early, x)
+    received = partner(other, "c")
+    (own,) = call(
+        own_kernel,
+        [flat],
+        [SMEM, SMEM, pl.BlockSpec((1, kinds, 2 * rank, LANES), lambda i: (3, 0, 0, 0)), VMEM],
+        cost=pl.CostEstimate(flops=2**24, bytes_accessed=2**20, transcendentals=0),
+    )(sources, types, early, left)
+    (x,) = call(end_kernel, [flat], [SMEM, SMEM, VMEM, VMEM, VMEM], [held, held])(sources, types, late, own, received)
+    steps = 3
+    (out,) = call(
+        root_kernel,
+        [jax.ShapeDtypeStruct((waves, blocks * width), F32)],
+        [
+            pl.BlockSpec(flat.shape, lambda i: (0, 0)),
+            pl.BlockSpec((blocks // steps, 4 * rank, width), lambda i: (i, 0, 0)),
+        ],
+        out_specs=[pl.BlockSpec((waves, blocks // steps * width), lambda i: (0, i))],
+        steps=steps,
+    )(exchange(x), root_weights)
     return out
 
 

time: 80.1 us -> 80.8 us (level)
  Pallas kernels: 18.2 us -> 20.2 us
  waiting for transfers between devices: 4.89 us -> 3.55 us
    ppermute x2, waiting for transfers between devices: 4.89 us -> 3.55 us  [partner(): return lax.ppermute(x, axis, [(0, 1), (1, 0)])]
    pallas_call x2 -> x3, Pallas kernels: 7.89 us -> 9.16 us  [the longest x1 4.14 us: local(): call(middle_kernel, [flat, jax.ShapeDtypeStruct((blocks, waves, LANES), B...]
  transfers between devices with their start and end apart: 2 -> 2, of which waited for: 2 -> 1; matrix products, arithmetic and copies ran while one was open for 0% -> 0% of each run, Pallas kernels for 4% -> 6%
where the time goes in v5:
time: 80.8 us; the launch traced here: 80.5 us
  blocking collectives  50 us (62%)
  Pallas kernels  20.2 us (25%)
  starting transfers between devices  5.6 us (7%)
  waiting for transfers between devices  3.55 us (4%)
  local copies, waits for them, and re-layouts  1 us (1%)
    all_to_all x2, blocking collectives, exchange(): return lax.all_to_all(x, GROUP, 0, 0, tiled=True).reshape(rows, LANES)  50 us
    ppermute x2, starting transfers between devices, partner(): return lax.ppermute(x, axis, [(0, 1), (1, 0)])  5.6 us
    pallas_call x1, Pallas kernels, local(): call(start_kernel, [flat, jax.ShapeDtypeStruct((blocks, waves, LANES), BF...  5.45 us
    pallas_call x1, Pallas kernels, local(): call(middle_kernel, [flat, jax.ShapeDtypeStruct((blocks, waves, LANES), B...  4.14 us
    pallas_call x1, Pallas kernels, local(): call(end_kernel, [flat], [SMEM, SMEM, VMEM, VMEM, VMEM], [held, held])  3.64 us
    ppermute x2, waiting for transfers between devices, partner(): return lax.ppermute(x, axis, [(0, 1), (1, 0)])  3.55 us
    pallas_call x1, Pallas kernels, local(): call(prepare_kernel, [flat, prepared(4), prepared(3), jax.ShapeDtypeStruc...  3.43 us
    pallas_call x1, Pallas kernels, local(): call(root_kernel, [jax.ShapeDtypeStruct((waves, blocks * width), F32)], [...  1.96 us
  transfers between devices with their start and end apart: 2, of which 1 were waited for; matrix products, arithmetic and copies ran while one was open for 0% of the time, Pallas kernels for 6%

profile of v5, /device:TPU:1, one launch (start us, length us, event | category | flops | bytes accessed | tf_op | source)
XLA Modules:
  0.0 80.5 jit_solution(14811208536964232771)
XLA Ops:
  0.0 0.0 copy-start
  0.0 0.0 copy-start.3
  0.0 0.0 copy-start.2
  0.0 0.0 copy-start.1
  0.0 5.5 %shard_map.64 = (f32[768,128]{1,0:T(8,128)}, bf16[24,64,128]{2,1,0:T(8,128)(2,1)}) custom-call(s32[8,4,24]{2,1,0:T(4,128)} %bitcast.11, s32[8,4,24]{2,1,0:T(4,128)} %bitcast.16, f32[8,8,64,64]{3,2,1,0:T(8,128)} %tables.3, f32[64,3072]{1,0:T(8,128)} %signals.1, f32[24,64,128]{2,1,0:T(8,128)} %maps.1), custom_call_target="tpu_custom_call" | custom-call | tf_op jit(solution)/shard_map/pallas_call | solution.py:275
  5.5 2.2 %collective-permute-start = (f32[768,128]{1,0:T(8,128)}, f32[768,128]{1,0:T(8,128)S(1)}, u32[]{:S(2)}, u32[]{:S(2)}) collective-permute-start(f32[768,128]{1,0:T(8,128)} %get-tuple-element.19), channel_id=1, source_target_pairs={{0,16},{16,0},{1,17},{17,1},{2,18},{18,2},{3,19},{19,3},{4,20},{20... | collective-permute-start | bytes 1179656 | tf_op jit(solution)/shard_map/ppermute | solution.py:264
  7.7 0.0 copy-done
  7.7 0.0 copy-done.3
  7.7 0.0 copy-done.2
  7.7 0.0 copy-done.1
  7.7 0.0 copy-start.4
  7.7 1.0 %copy-done.4 = bf16[24,64,128]{2,1,0:T(8,128)(2,1)S(1)} copy-done((bf16[24,64,128]{2,1,0:T(8,128)(2,1)S(1)}, bf16[24,64,128]{2,1,0:T(8,128)(2,1)}, u32[]{:S(2)}) %copy-start.4) | copy-done | bytes 393240
  8.7 3.4 %shard_map.65 = (f32[768,128]{1,0:T(8,128)S(1)}, bf16[4,8,128,128]{3,2,1,0:T(8,128)(2,1)S(1)}, bf16[3,8,128,128]{3,2,1,0:T(8,128)(2,1)S(1)}, bf16[24,256,128]{2,1,0:T(8,128)(2,1)S(1)}) custom-call(s32[8,4,24]{2,1,0:T(4,128)S(1)} %bitcast.12, s32[8,4,24]{2,1,0:T(4,128)S(1)} %bitcast.17, f32[8,8,64,64]{3,2,1,0:T(8,128)S(1)} %copy-done, ...), custom_call_target="tpu_custom_call" | custom-call | flops 16777216 | bytes 8388608 | tf_op jit(solution)/shard_map/pallas_call | solution.py:295
  12.1 3.5 %collective-permute-done = f32[768,128]{1,0:T(8,128)S(1)} collective-permute-done((f32[768,128]{1,0:T(8,128)}, f32[768,128]{1,0:T(8,128)S(1)}, u32[]{:S(2)}, u32[]{:S(2)}) %collective-permute-start) | collective-permute-done | bytes 393248 | tf_op jit(solution)/shard_map/ppermute | solution.py:264
  15.7 29.4 %all_to_all.10 = f32[64,1,1536]{2,1,0:T(1,128)S(1)} all-to-all(f32[64,1,1536]{2,1,0:T(1,128)S(1)} %bitcast.21), channel_id=1, replica_groups=mesh['z1'=2,'z0'=2,'y1'=2,'y0'=2,'x1'=2,'x0'=2,'zh'=2,'c'=2] {'z1','z0',..., dimensions={0} | all-to-all | bytes 786432 | tf_op jit(solution)/shard_map/all_to_all | solution.py:260
  45.1 4.1 %shard_map.66 = (f32[768,128]{1,0:T(8,128)S(1)}, bf16[24,64,128]{2,1,0:T(8,128)(2,1)S(1)}) custom-call(s32[8,4,24]{2,1,0:T(4,128)S(1)} %bitcast.13, s32[8,4,24]{2,1,0:T(4,128)S(1)} %bitcast.18, bf16[4,8,128,128]{3,2,1,0:T(8,128)(2,1)S(1)} %get-tuple-element.24.weights, f32[768,128]{1,0:T(8,128)S(1)} %bitcast.7), custom_call_target="tpu_custom_call" | custom-call | tf_op jit(solution)/shard_map/pallas_call | solution.py:304
  49.2 3.4 %collective-permute-start.1 = (f32[768,128]{1,0:T(8,128)S(1)}, f32[768,128]{1,0:T(8,128)S(1)}, u32[]{:S(2)}, u32[]{:S(2)}) collective-permute-start(f32[768,128]{1,0:T(8,128)S(1)} %get-tuple-element.27), channel_id=1, source_target_pairs={{0,1},{1,0},{2,3},{3,2},{4,5},{5,4},{6,7},{7,6},{8,9},{9,8},{10,11... | collective-permute-start | bytes 1179656 | tf_op jit(solution)/shard_map/ppermute | solution.py:264
  52.6 1.6 %shard_map.67.own_ref = f32[768,128]{1,0:T(8,128)S(1)} custom-call(s32[8,4,24]{2,1,0:T(4,128)S(1)} %bitcast.14, s32[8,4,24]{2,1,0:T(4,128)S(1)} %bitcast.19, bf16[4,8,128,128]{3,2,1,0:T(8,128)(2,1)S(1)} %get-tuple-element.24.weights, bf16[24,64,128]{2,1,0:T(8,128)(2,1)S(1)} %get-tuple-element.26.left), custom_call_target="tpu_custom_call" | custom-call | flops 16777216 | bytes 1048576 | tf_op jit(solution)/shard_map/pallas_call | solution.py:311
  54.2 0.0 collective-permute-done.1.other_ref
  54.2 3.6 %shard_map.68 = f32[768,128]{1,0:T(8,128)S(1)} custom-call(s32[8,4,24]{2,1,0:T(4,128)S(1)} %bitcast.15, s32[8,4,24]{2,1,0:T(4,128)S(1)} %bitcast.20, bf16[3,8,128,128]{3,2,1,0:T(8,128)(2,1)S(1)} %get-tuple-element.23.weights, f32[768,128]{1,0:T(8,128)S(1)} %shard_map.67.own_ref, f32[768,128]{1,0:T(8,128)S(1)} %collective-permute-done.1.other_ref), custom_call_target="tpu_custom_call" | custom-call | tf_op jit(solution)/shard_map/pallas_call | solution.py:317
  57.9 20.7 %all_to_all.11 = f32[64,1,1536]{2,1,0:T(1,128)S(1)} all-to-all(f32[64,1,1536]{2,1,0:T(1,128)S(1)} %bitcast.8), channel_id=1, replica_groups=mesh['z1'=2,'z0'=2,'y1'=2,'y0'=2,'x1'=2,'x0'=2,'zh'=2,'c'=2] {'z1','z0',..., dimensions={0} | all-to-all | bytes 786432 | tf_op jit(solution)/shard_map/all_to_all | solution.py:260
  78.5 2.0 %shard_map.69 = f32[64,3072]{1,0:T(8,128)} custom-call(f32[768,128]{1,0:T(8,128)S(1)} %bitcast.9, bf16[24,256,128]{2,1,0:T(8,128)(2,1)S(1)} %get-tuple-element.28.weights), custom_call_target="tpu_custom_call" | custom-call | tf_op jit(solution)/shard_map/pallas_call | solution.py:319
  (1 shorter events, 0.0 us)
Async XLA Ops:
  0.0 7.7 %copy-start = (f32[8,8,64,64]{3,2,1,0:T(8,128)S(1)}, f32[8,8,64,64]{3,2,1,0:T(8,128)}, u32[]{:S(2)}) copy-start(f32[8,8,64,64]{3,2,1,0:T(8,128)} %tables.3) | copy-start | bytes 3145732
  0.0 7.7 %copy-start.3 = (s32[8,24,4]{1,2,0:T(4,128)S(1)}, s32[8,24,4]{1,2,0:T(4,128)}, u32[]{:S(2)}) copy-start(s32[8,24,4]{1,2,0:T(4,128)} %param.11) | copy-start | bytes 9220
  0.0 7.7 %copy-start.2 = (s32[8,24,4]{1,2,0:T(4,128)S(1)}, s32[8,24,4]{1,2,0:T(4,128)}, u32[]{:S(2)}) copy-start(s32[8,24,4]{1,2,0:T(4,128)} %param.10) | copy-start | bytes 9220
  0.0 7.7 %copy-start.1 = (f32[24,128,64]{1,2,0:T(8,128)S(1)}, f32[24,128,64]{1,2,0:T(8,128)}, u32[]{:S(2)}) copy-start(f32[24,128,64]{1,2,0:T(8,128)} %param.8) | copy-start | bytes 2359300
  5.5 10.2 %collective-permute-start = (f32[768,128]{1,0:T(8,128)}, f32[768,128]{1,0:T(8,128)S(1)}, u32[]{:S(2)}, u32[]{:S(2)}) collective-permute-start(f32[768,128]{1,0:T(8,128)} %get-tuple-element.19), channel_id=1, source_target_pairs={{0,16},{16,0},{1,17},{17,1},{2,18},{18,2},{3,19},{19,3},{4,20},{20... | collective-permute-start | bytes 1179656 | tf_op jit(solution)/shard_map/ppermute | solution.py:264
  7.7 1.0 %copy-start.4 = (bf16[24,64,128]{2,1,0:T(8,128)(2,1)S(1)}, bf16[24,64,128]{2,1,0:T(8,128)(2,1)}, u32[]{:S(2)}) copy-start(bf16[24,64,128]{2,1,0:T(8,128)(2,1)} %get-tuple-element.17.held) | copy-start | bytes 1179652
  49.2 5.0 %collective-permute-start.1 = (f32[768,128]{1,0:T(8,128)S(1)}, f32[768,128]{1,0:T(8,128)S(1)}, u32[]{:S(2)}, u32[]{:S(2)}) collective-permute-start(f32[768,128]{1,0:T(8,128)S(1)} %get-tuple-element.27), channel_id=1, source_target_pairs={{0,1},{1,0},{2,3},{3,2},{4,5},{5,4},{6,7},{7,6},{8,9},{9,8},{10,11... | collective-permute-start | bytes 1179656 | tf_op jit(solution)/shard_map/ppermute | solution.py:264

commit v6 on v5

--- a/solution.py
+++ b/solution.py
@@ -141,7 +141,7 @@
 
 
 def start_kernel(
-    sources, types, tables, signals, maps, other_ref, left_ref, held, weights, table_in, signals_in, maps_in, sems
+    sources, types, tables, signals, maps, other_ref, held, weights, table_in, signals_in, maps_in, sems
 ):
     blocks, rank, width = maps.shape
     parts = sems.shape[1]
@@ -176,10 +176,7 @@
         for copy in copies[i]:
             copy.wait()
         lax.fori_loop(i * some, (i + 1) * some, leaf, 0, unroll=some)
-    left_copy = pltpu.make_async_copy(held, left_ref, sems.at[2, 1])
-    left_copy.start()
     half_level(0, 2, blocks, sources, types, held, weights, other_ref)
-    left_copy.wait()
 
 
 def prepare_kernel(sources, types, tables, maps, held, own_ref, early, late, root_weights, weights_here):
@@ -225,15 +222,18 @@
 
 def root_kernel(x_ref, weights, out_ref):
     blocks, width = weights.shape[0], weights.shape[2]
-    first = pl.program_id(0) * (blocks // 2)
-    for pair in range(blocks // 2):
-        x = x_ref[pair_rows(x_ref, first + pair), :]
+
+    def body(pair, carry):
+        x = x_ref[pair_rows(x_ref, pair), :]
         turned = turn(x)
         low = low_lanes(x.shape)
         for block, value in ((2 * pair, jnp.where(low, x, turned)), (2 * pair + 1, jnp.where(low, turned, x))):
             left = hi_lo_lanes(value)
             out = jnp.dot(jnp.concatenate([left, left], axis=1), weights[block], preferred_element_type=F32)
-            out_ref[:, block * width : (block + 1) * width] = out
+            out_ref[:, pl.ds(pl.multiple_of(block * width, width), width)] = out
+        return carry
+
+    lax.fori_loop(0, blocks // 2, body, 0, unroll=4)
 
 
 VMEM = pl.BlockSpec(memory_space=pltpu.VMEM)
@@ -241,13 +241,13 @@
 HBM = pl.BlockSpec(memory_space=pltpu.HBM)
 
 
-def call(kernel, outs, specs, scratch=(), mib=12, cost=None, out_specs=None, steps=1):
+def call(kernel, outs, specs, scratch=(), mib=12, cost=None):
     return pl.pallas_call(
         kernel,
         out_shape=outs,
-        grid=(steps,),
+        grid=(1,),
         in_specs=specs,
-        out_specs=out_specs or [VMEM] * len(outs),
+        out_specs=[VMEM] * len(outs),
         scratch_shapes=scratch,
         cost_estimate=cost,
         compiler_params=pltpu.CompilerParams(vmem_limit_bytes=mib * 2**20),
@@ -277,7 +277,6 @@
         [flat, jax.ShapeDtypeStruct((blocks, waves, LANES), BF16)],
         [SMEM, SMEM, HBM, HBM, HBM],
         [
-            held,
             pltpu.VMEM((kinds, 2 * rank, LANES), BF16),
             pltpu.VMEM((kinds, rank, rank), F32),
             pltpu.VMEM((waves, blocks * width), F32),
@@ -285,8 +284,8 @@
             pltpu.SemaphoreType.DMA((3, 3)),
         ],
         mib=60,
-        out_specs=[VMEM, HBM],
     )(sources, types, translations, signals, leaf_maps)
+    other, translations, root_maps = lax.optimization_barrier((other, translations, root_maps))
     received = partner(other, "y0")
 
     def prepared(count):
@@ -315,17 +314,9 @@
         cost=pl.CostEstimate(flops=2**24, bytes_accessed=2**20, transcendentals=0),
     )(sources, types, early, left)
     (x,) = call(end_kernel, [flat], [SMEM, SMEM, VMEM, VMEM, VMEM], [held, held])(sources, types, late, own, received)
-    steps = 3
-    (out,) = call(
-        root_kernel,
-        [jax.ShapeDtypeStruct((waves, blocks * width), F32)],
-        [
-            pl.BlockSpec(flat.shape, lambda i: (0, 0)),
-            pl.BlockSpec((blocks // steps, 4 * rank, width), lambda i: (i, 0, 0)),
-        ],
-        out_specs=[pl.BlockSpec((waves, blocks // steps * width), lambda i: (0, i))],
-        steps=steps,
-    )(exchange(x), root_weights)
+    (out,) = call(root_kernel, [jax.ShapeDtypeStruct((waves, blocks * width), F32)], [VMEM, VMEM])(
+        exchange(x), root_weights
+    )
     return out
 
 

time: 80.8 us -> 80 us (0.990)
  no operation moved by 1% of the time
where the time goes in v6:
time: 80 us; the launch traced here: 79.7 us
  blocking collectives  50.1 us (63%)
  Pallas kernels  19.4 us (24%)
  starting transfers between devices  5.6 us (7%)
  waiting for transfers between devices  3.55 us (4%)
  local copies, waits for them, and re-layouts  1 us (1%)
    all_to_all x2, blocking collectives, exchange(): return lax.all_to_all(x, GROUP, 0, 0, tiled=True).reshape(rows, LANES)  50.1 us
    ppermute x2, starting transfers between devices, partner(): return lax.ppermute(x, axis, [(0, 1), (1, 0)])  5.6 us
    pallas_call x1, Pallas kernels, local(): call(start_kernel, [flat, jax.ShapeDtypeStruct((blocks, waves, LANES), BF...  4.93 us
    pallas_call x1, Pallas kernels, local(): call(middle_kernel, [flat, jax.ShapeDtypeStruct((blocks, waves, LANES), B...  4.14 us
    pallas_call x1, Pallas kernels, local(): call(end_kernel, [flat], [SMEM, SMEM, VMEM, VMEM, VMEM], [held, held])  3.63 us
    ppermute x2, waiting for transfers between devices, partner(): return lax.ppermute(x, axis, [(0, 1), (1, 0)])  3.55 us
    pallas_call x1, Pallas kernels, local(): call(prepare_kernel, [flat, prepared(4), prepared(3), jax.ShapeDtypeStruc...  3.43 us
    pallas_call x1, Pallas kernels, local(): call(root_kernel, [jax.ShapeDtypeStruct((waves, blocks * width), F32)], [...  1.71 us
  transfers between devices with their start and end apart: 2, of which 1 were waited for; matrix products, arithmetic and copies ran while one was open for 0% of the time, Pallas kernels for 6%

profile of v6, /device:TPU:1, one launch (start us, length us, event | category | flops | bytes accessed | tf_op | source)
XLA Modules:
  0.0 79.7 jit_solution(11370460253195811937)
XLA Ops:
  0.0 0.0 copy-start
  0.0 0.0 copy-start.3
  0.0 0.0 copy-start.2
  0.0 0.0 copy-start.1
  0.0 4.9 %shard_map.64 = (f32[768,128]{1,0:T(8,128)}, bf16[24,64,128]{2,1,0:T(8,128)(2,1)}) custom-call(s32[8,4,24]{2,1,0:T(4,128)} %bitcast.11, s32[8,4,24]{2,1,0:T(4,128)} %bitcast.16, f32[8,8,64,64]{3,2,1,0:T(8,128)} %tables.2, f32[64,3072]{1,0:T(8,128)} %signals.1, f32[24,64,128]{2,1,0:T(8,128)} %maps.1), custom_call_target="tpu_custom_call" | custom-call | tf_op jit(solution)/shard_map/pallas_call | solution.py:275
  5.0 2.2 %collective-permute-start = (f32[768,128]{1,0:T(8,128)}, f32[768,128]{1,0:T(8,128)S(1)}, u32[]{:S(2)}, u32[]{:S(2)}) collective-permute-start(f32[768,128]{1,0:T(8,128)} %get-tuple-element.25), channel_id=1, source_target_pairs={{0,16},{16,0},{1,17},{17,1},{2,18},{18,2},{3,19},{19,3},{4,20},{20... | collective-permute-start | bytes 1179656 | tf_op jit(solution)/shard_map/ppermute | solution.py:264
  7.2 0.0 copy-done
  7.2 0.0 copy-done.3
  7.2 0.0 copy-done.2
  7.2 0.0 copy-done.1
  7.2 0.0 copy-start.4
  7.2 1.0 %copy-done.4 = bf16[24,64,128]{2,1,0:T(8,128)(2,1)S(1)} copy-done((bf16[24,64,128]{2,1,0:T(8,128)(2,1)S(1)}, bf16[24,64,128]{2,1,0:T(8,128)(2,1)}, u32[]{:S(2)}) %copy-start.4) | copy-done | bytes 393240
  8.2 3.4 %shard_map.65 = (f32[768,128]{1,0:T(8,128)S(1)}, bf16[4,8,128,128]{3,2,1,0:T(8,128)(2,1)S(1)}, bf16[3,8,128,128]{3,2,1,0:T(8,128)(2,1)S(1)}, bf16[24,256,128]{2,1,0:T(8,128)(2,1)S(1)}) custom-call(s32[8,4,24]{2,1,0:T(4,128)S(1)} %bitcast.12, s32[8,4,24]{2,1,0:T(4,128)S(1)} %bitcast.17, f32[8,8,64,64]{3,2,1,0:T(8,128)S(1)} %copy-done, ...), custom_call_target="tpu_custom_call" | custom-call | flops 16777216 | bytes 8388608 | tf_op jit(solution)/shard_map/pallas_call | solution.py:294
  11.6 3.5 %collective-permute-done = f32[768,128]{1,0:T(8,128)S(1)} collective-permute-done((f32[768,128]{1,0:T(8,128)}, f32[768,128]{1,0:T(8,128)S(1)}, u32[]{:S(2)}, u32[]{:S(2)}) %collective-permute-start) | collective-permute-done | bytes 393248 | tf_op jit(solution)/shard_map/ppermute | solution.py:264
  15.2 29.4 %all_to_all.10 = f32[64,1,1536]{2,1,0:T(1,128)S(1)} all-to-all(f32[64,1,1536]{2,1,0:T(1,128)S(1)} %bitcast.21), channel_id=1, replica_groups=mesh['z1'=2,'z0'=2,'y1'=2,'y0'=2,'x1'=2,'x0'=2,'zh'=2,'c'=2] {'z1','z0',..., dimensions={0} | all-to-all | bytes 786432 | tf_op jit(solution)/shard_map/all_to_all | solution.py:260
  44.6 4.1 %shard_map.66 = (f32[768,128]{1,0:T(8,128)S(1)}, bf16[24,64,128]{2,1,0:T(8,128)(2,1)S(1)}) custom-call(s32[8,4,24]{2,1,0:T(4,128)S(1)} %bitcast.13, s32[8,4,24]{2,1,0:T(4,128)S(1)} %bitcast.18, bf16[4,8,128,128]{3,2,1,0:T(8,128)(2,1)S(1)} %get-tuple-element.30.weights, f32[768,128]{1,0:T(8,128)S(1)} %bitcast.7), custom_call_target="tpu_custom_call" | custom-call | tf_op jit(solution)/shard_map/pallas_call | solution.py:303
  48.7 3.4 %collective-permute-start.1 = (f32[768,128]{1,0:T(8,128)S(1)}, f32[768,128]{1,0:T(8,128)S(1)}, u32[]{:S(2)}, u32[]{:S(2)}) collective-permute-start(f32[768,128]{1,0:T(8,128)S(1)} %get-tuple-element.33), channel_id=1, source_target_pairs={{0,1},{1,0},{2,3},{3,2},{4,5},{5,4},{6,7},{7,6},{8,9},{9,8},{10,11... | collective-permute-start | bytes 1179656 | tf_op jit(solution)/shard_map/ppermute | solution.py:264
  52.1 1.6 %shard_map.67.own_ref = f32[768,128]{1,0:T(8,128)S(1)} custom-call(s32[8,4,24]{2,1,0:T(4,128)S(1)} %bitcast.14, s32[8,4,24]{2,1,0:T(4,128)S(1)} %bitcast.19, bf16[4,8,128,128]{3,2,1,0:T(8,128)(2,1)S(1)} %get-tuple-element.30.weights, bf16[24,64,128]{2,1,0:T(8,128)(2,1)S(1)} %get-tuple-element.32.left), custom_call_target="tpu_custom_call" | custom-call | flops 16777216 | bytes 1048576 | tf_op jit(solution)/shard_map/pallas_call | solution.py:310
  53.7 0.0 collective-permute-done.1.other_ref
  53.7 3.6 %shard_map.68 = f32[768,128]{1,0:T(8,128)S(1)} custom-call(s32[8,4,24]{2,1,0:T(4,128)S(1)} %bitcast.15, s32[8,4,24]{2,1,0:T(4,128)S(1)} %bitcast.20, bf16[3,8,128,128]{3,2,1,0:T(8,128)(2,1)S(1)} %get-tuple-element.29.weights, f32[768,128]{1,0:T(8,128)S(1)} %shard_map.67.own_ref, f32[768,128]{1,0:T(8,128)S(1)} %collective-permute-done.1.other_ref), custom_call_target="tpu_custom_call" | custom-call | tf_op jit(solution)/shard_map/pallas_call | solution.py:316
  57.3 20.7 %all_to_all.11 = f32[64,1,1536]{2,1,0:T(1,128)S(1)} all-to-all(f32[64,1,1536]{2,1,0:T(1,128)S(1)} %bitcast.8), channel_id=1, replica_groups=mesh['z1'=2,'z0'=2,'y1'=2,'y0'=2,'x1'=2,'x0'=2,'zh'=2,'c'=2] {'z1','z0',..., dimensions={0} | all-to-all | bytes 786432 | tf_op jit(solution)/shard_map/all_to_all | solution.py:260
  78.0 1.7 %shard_map.69 = f32[64,3072]{1,0:T(8,128)} custom-call(f32[768,128]{1,0:T(8,128)S(1)} %bitcast.9, bf16[24,256,128]{2,1,0:T(8,128)(2,1)S(1)} %get-tuple-element.34.weights), custom_call_target="tpu_custom_call" | custom-call | tf_op jit(solution)/shard_map/pallas_call | solution.py:317
  (1 shorter events, 0.0 us)
Async XLA Ops:
  0.0 7.2 %copy-start = (f32[8,8,64,64]{3,2,1,0:T(8,128)S(1)}, f32[8,8,64,64]{3,2,1,0:T(8,128)}, u32[]{:S(2)}) copy-start(f32[8,8,64,64]{3,2,1,0:T(8,128)} %tables.2) | copy-start | bytes 3145732
  0.0 7.2 %copy-start.3 = (s32[8,24,4]{1,2,0:T(4,128)S(1)}, s32[8,24,4]{1,2,0:T(4,128)}, u32[]{:S(2)}) copy-start(s32[8,24,4]{1,2,0:T(4,128)} %param.11) | copy-start | bytes 9220
  0.0 7.2 %copy-start.2 = (s32[8,24,4]{1,2,0:T(4,128)S(1)}, s32[8,24,4]{1,2,0:T(4,128)}, u32[]{:S(2)}) copy-start(s32[8,24,4]{1,2,0:T(4,128)} %param.10) | copy-start | bytes 9220
  0.0 7.2 %copy-start.1 = (f32[24,128,64]{1,2,0:T(8,128)S(1)}, f32[24,128,64]{1,2,0:T(8,128)}, u32[]{:S(2)}) copy-start(f32[24,128,64]{1,2,0:T(8,128)} %param.8) | copy-start | bytes 2359300
  5.0 10.2 %collective-permute-start = (f32[768,128]{1,0:T(8,128)}, f32[768,128]{1,0:T(8,128)S(1)}, u32[]{:S(2)}, u32[]{:S(2)}) collective-permute-start(f32[768,128]{1,0:T(8,128)} %get-tuple-element.25), channel_id=1, source_target_pairs={{0,16},{16,0},{1,17},{17,1},{2,18},{18,2},{3,19},{19,3},{4,20},{20... | collective-permute-start | bytes 1179656 | tf_op jit(solution)/shard_map/ppermute | solution.py:264
  7.2 1.0 %copy-start.4 = (bf16[24,64,128]{2,1,0:T(8,128)(2,1)S(1)}, bf16[24,64,128]{2,1,0:T(8,128)(2,1)}, u32[]{:S(2)}) copy-start(bf16[24,64,128]{2,1,0:T(8,128)(2,1)} %get-tuple-element.23.held) | copy-start | bytes 1179652
  48.7 5.0 %collective-permute-start.1 = (f32[768,128]{1,0:T(8,128)S(1)}, f32[768,128]{1,0:T(8,128)S(1)}, u32[]{:S(2)}, u32[]{:S(2)}) collective-permute-start(f32[768,128]{1,0:T(8,128)S(1)} %get-tuple-element.33), channel_id=1, source_target_pairs={{0,1},{1,0},{2,3},{3,2},{4,5},{5,4},{6,7},{7,6},{8,9},{9,8},{10,11... | collective-permute-start | bytes 1179656 | tf_op jit(solution)/shard_map/ppermute | solution.py:264

commit v7 on v6

--- a/solution.py
+++ b/solution.py
@@ -66,15 +66,13 @@
 
 def put_weights(mat, out_ref):
     hi, lo = split(mat.T)
-    both = jnp.concatenate([hi, lo], axis=1)
-    rank = mat.shape[0]
-    out_ref[:rank] = both
-    out_ref[rank:] = both
+    out_ref[...] = jnp.concatenate([hi, lo], axis=1)
 
 
 def two_terms(level, block, entry, sources, types, back, held, weights):
     left = [held[sources[level, entry + i, block] - back] for i in range(2)]
     right = [weights[types[level, entry + i, block]] for i in range(2)]
+    right = [right[0], right[0], right[1], right[1]]
     return jnp.dot(jnp.concatenate(left, axis=1), jnp.concatenate(right, axis=0), preferred_element_type=F32)
 
 
@@ -195,7 +193,7 @@
 
     def root(block, carry):
         hi, lo = split(maps[block])
-        root_weights[block] = jnp.concatenate([hi, hi, lo, lo], axis=0)
+        root_weights[block] = jnp.concatenate([hi, lo], axis=0)
         return carry
 
     lax.fori_loop(0, maps.shape[0], root, 0, unroll=4)
@@ -221,7 +219,7 @@
 
 
 def root_kernel(x_ref, weights, out_ref):
-    blocks, width = weights.shape[0], weights.shape[2]
+    blocks, rank, width = weights.shape[0], weights.shape[1] // 2, weights.shape[2]
 
     def body(pair, carry):
         x = x_ref[pair_rows(x_ref, pair), :]
@@ -229,7 +227,9 @@
         low = low_lanes(x.shape)
         for block, value in ((2 * pair, jnp.where(low, x, turned)), (2 * pair + 1, jnp.where(low, turned, x))):
             left = hi_lo_lanes(value)
-            out = jnp.dot(jnp.concatenate([left, left], axis=1), weights[block], preferred_element_type=F32)
+            hi, lo = weights[block, :rank], weights[block, rank:]
+            right = jnp.concatenate([hi, hi, lo, lo], axis=0)
+            out = jnp.dot(jnp.concatenate([left, left], axis=1), right, preferred_element_type=F32)
             out_ref[:, pl.ds(pl.multiple_of(block * width, width), width)] = out
         return carry
 
@@ -277,7 +277,7 @@
         [flat, jax.ShapeDtypeStruct((blocks, waves, LANES), BF16)],
         [SMEM, SMEM, HBM, HBM, HBM],
         [
-            pltpu.VMEM((kinds, 2 * rank, LANES), BF16),
+            pltpu.VMEM((kinds, rank, LANES), BF16),
             pltpu.VMEM((kinds, rank, rank), F32),
             pltpu.VMEM((waves, blocks * width), F32),
             pltpu.VMEM((blocks, rank, width), F32),
@@ -289,13 +289,13 @@
     received = partner(other, "y0")
 
     def prepared(count):
-        return jax.ShapeDtypeStruct((count, kinds, 2 * rank, LANES), BF16)
+        return jax.ShapeDtypeStruct((count, kinds, rank, LANES), BF16)
 
     own, early, late, root_weights = call(
         prepare_kernel,
-        [flat, prepared(4), prepared(3), jax.ShapeDtypeStruct((blocks, 4 * rank, width), BF16)],
+        [flat, prepared(4), prepared(3), jax.ShapeDtypeStruct((blocks, 2 * rank, width), BF16)],
         [SMEM, SMEM, VMEM, VMEM, VMEM],
-        [pltpu.VMEM((kinds, 2 * rank, LANES), BF16)],
+        [pltpu.VMEM((kinds, rank, LANES), BF16)],
         cost=pl.CostEstimate(flops=2**24, bytes_accessed=2**23, transcendentals=0),
     )(sources, types, translations, root_maps, left)
     x, early, late, root_weights = lax.optimization_barrier((own + received, early, late, root_weights))
@@ -310,7 +310,7 @@
     (own,) = call(
         own_kernel,
         [flat],
-        [SMEM, SMEM, pl.BlockSpec((1, kinds, 2 * rank, LANES), lambda i: (3, 0, 0, 0)), VMEM],
+        [SMEM, SMEM, pl.BlockSpec((1, kinds, rank, LANES), lambda i: (3, 0, 0, 0)), VMEM],
         cost=pl.CostEstimate(flops=2**24, bytes_accessed=2**20, transcendentals=0),
     )(sources, types, early, left)
     (x,) = call(end_kernel, [flat], [SMEM, SMEM, VMEM, VMEM, VMEM], [held, held])(sources, types, late, own, received)

time: 80 us -> 79 us (0.988)
  Pallas kernels: 19.4 us -> 18.3 us
where the time goes in v7:
time: 79 us; the launch traced here: 78.7 us
  blocking collectives  50.1 us (63%)
  Pallas kernels  18.3 us (23%)
  starting transfers between devices  5.6 us (7%)
  waiting for transfers between devices  3.66 us (5%)
  local copies, waits for them, and re-layouts  1 us (1%)
    all_to_all x2, blocking collectives, exchange(): return lax.all_to_all(x, GROUP, 0, 0, tiled=True).reshape(rows, LANES)  50.1 us
    ppermute x2, starting transfers between devices, partner(): return lax.ppermute(x, axis, [(0, 1), (1, 0)])  5.6 us
    pallas_call x1, Pallas kernels, local(): call(start_kernel, [flat, jax.ShapeDtypeStruct((blocks, waves, LANES), BF...  4.87 us
    ppermute x2, waiting for transfers between devices, partner(): return lax.ppermute(x, axis, [(0, 1), (1, 0)])  3.66 us
    pallas_call x1, Pallas kernels, local(): call(middle_kernel, [flat, jax.ShapeDtypeStruct((blocks, waves, LANES), B...  3.6 us
    pallas_call x1, Pallas kernels, local(): call(prepare_kernel, [flat, prepared(4), prepared(3), jax.ShapeDtypeStruc...  3.32 us
    pallas_call x1, Pallas kernels, local(): call(end_kernel, [flat], [SMEM, SMEM, VMEM, VMEM, VMEM], [held, held])  3.23 us
    pallas_call x1, Pallas kernels, local(): call(root_kernel, [jax.ShapeDtypeStruct((waves, blocks * width), F32)], [...  1.72 us
  transfers between devices with their start and end apart: 2, of which 1 were waited for; matrix products, arithmetic and copies ran while one was open for 0% of the time, Pallas kernels for 6%

profile of v7, /device:TPU:1, one launch (start us, length us, event | category | flops | bytes accessed | tf_op | source)
XLA Modules:
  0.0 78.7 jit_solution(9914177482364862292)
XLA Ops:
  0.0 0.0 copy-start
  0.0 0.0 copy-start.3
  0.0 0.0 copy-start.2
  0.0 0.0 copy-start.1
  0.0 4.9 %shard_map.64 = (f32[768,128]{1,0:T(8,128)}, bf16[24,64,128]{2,1,0:T(8,128)(2,1)}) custom-call(s32[8,4,24]{2,1,0:T(4,128)} %bitcast.11, s32[8,4,24]{2,1,0:T(4,128)} %bitcast.16, f32[8,8,64,64]{3,2,1,0:T(8,128)} %tables.2, f32[64,3072]{1,0:T(8,128)} %signals.1, f32[24,64,128]{2,1,0:T(8,128)} %maps.1), custom_call_target="tpu_custom_call" | custom-call | tf_op jit(solution)/shard_map/pallas_call | solution.py:275
  4.9 2.2 %collective-permute-start = (f32[768,128]{1,0:T(8,128)}, f32[768,128]{1,0:T(8,128)S(1)}, u32[]{:S(2)}, u32[]{:S(2)}) collective-permute-start(f32[768,128]{1,0:T(8,128)} %get-tuple-element.25), channel_id=1, source_target_pairs={{0,16},{16,0},{1,17},{17,1},{2,18},{18,2},{3,19},{19,3},{4,20},{20... | collective-permute-start | bytes 1179656 | tf_op jit(solution)/shard_map/ppermute | solution.py:264
  7.1 0.0 copy-done
  7.1 0.0 copy-done.3
  7.1 0.0 copy-done.2
  7.1 0.0 copy-done.1
  7.1 0.0 copy-start.4
  7.1 1.0 %copy-done.4 = bf16[24,64,128]{2,1,0:T(8,128)(2,1)S(1)} copy-done((bf16[24,64,128]{2,1,0:T(8,128)(2,1)S(1)}, bf16[24,64,128]{2,1,0:T(8,128)(2,1)}, u32[]{:S(2)}) %copy-start.4) | copy-done | bytes 393240
  8.1 3.3 %shard_map.65 = (f32[768,128]{1,0:T(8,128)S(1)}, bf16[4,8,64,128]{3,2,1,0:T(8,128)(2,1)S(1)}, bf16[3,8,64,128]{3,2,1,0:T(8,128)(2,1)S(1)}, bf16[24,128,128]{2,1,0:T(8,128)(2,1)S(1)}) custom-call(s32[8,4,24]{2,1,0:T(4,128)S(1)} %bitcast.12, s32[8,4,24]{2,1,0:T(4,128)S(1)} %bitcast.17, f32[8,8,64,64]{3,2,1,0:T(8,128)S(1)} %copy-done, ...), custom_call_target="tpu_custom_call" | custom-call | flops 16777216 | bytes 8388608 | tf_op jit(solution)/shard_map/pallas_call | solution.py:294
  11.4 3.7 %collective-permute-done = f32[768,128]{1,0:T(8,128)S(1)} collective-permute-done((f32[768,128]{1,0:T(8,128)}, f32[768,128]{1,0:T(8,128)S(1)}, u32[]{:S(2)}, u32[]{:S(2)}) %collective-permute-start) | collective-permute-done | bytes 393248 | tf_op jit(solution)/shard_map/ppermute | solution.py:264
  15.1 29.4 %all_to_all.10 = f32[64,1,1536]{2,1,0:T(1,128)S(1)} all-to-all(f32[64,1,1536]{2,1,0:T(1,128)S(1)} %bitcast.21), channel_id=1, replica_groups=mesh['z1'=2,'z0'=2,'y1'=2,'y0'=2,'x1'=2,'x0'=2,'zh'=2,'c'=2] {'z1','z0',..., dimensions={0} | all-to-all | bytes 786432 | tf_op jit(solution)/shard_map/all_to_all | solution.py:260
  44.5 3.6 %shard_map.66 = (f32[768,128]{1,0:T(8,128)S(1)}, bf16[24,64,128]{2,1,0:T(8,128)(2,1)S(1)}) custom-call(s32[8,4,24]{2,1,0:T(4,128)S(1)} %bitcast.13, s32[8,4,24]{2,1,0:T(4,128)S(1)} %bitcast.18, bf16[4,8,64,128]{3,2,1,0:T(8,128)(2,1)S(1)} %get-tuple-element.30.weights, f32[768,128]{1,0:T(8,128)S(1)} %bitcast.7), custom_call_target="tpu_custom_call" | custom-call | tf_op jit(solution)/shard_map/pallas_call | solution.py:303
  48.1 3.4 %collective-permute-start.1 = (f32[768,128]{1,0:T(8,128)S(1)}, f32[768,128]{1,0:T(8,128)S(1)}, u32[]{:S(2)}, u32[]{:S(2)}) collective-permute-start(f32[768,128]{1,0:T(8,128)S(1)} %get-tuple-element.33), channel_id=1, source_target_pairs={{0,1},{1,0},{2,3},{3,2},{4,5},{5,4},{6,7},{7,6},{8,9},{9,8},{10,11... | collective-permute-start | bytes 1179656 | tf_op jit(solution)/shard_map/ppermute | solution.py:264
  51.5 1.5 %shard_map.67.own_ref = f32[768,128]{1,0:T(8,128)S(1)} custom-call(s32[8,4,24]{2,1,0:T(4,128)S(1)} %bitcast.14, s32[8,4,24]{2,1,0:T(4,128)S(1)} %bitcast.19, bf16[4,8,64,128]{3,2,1,0:T(8,128)(2,1)S(1)} %get-tuple-element.30.weights, bf16[24,64,128]{2,1,0:T(8,128)(2,1)S(1)} %get-tuple-element.32.left), custom_call_target="tpu_custom_call" | custom-call | flops 16777216 | bytes 1048576 | tf_op jit(solution)/shard_map/pallas_call | solution.py:310
  53.0 0.0 collective-permute-done.1.other_ref
  53.0 3.2 %shard_map.68 = f32[768,128]{1,0:T(8,128)S(1)} custom-call(s32[8,4,24]{2,1,0:T(4,128)S(1)} %bitcast.15, s32[8,4,24]{2,1,0:T(4,128)S(1)} %bitcast.20, bf16[3,8,64,128]{3,2,1,0:T(8,128)(2,1)S(1)} %get-tuple-element.29.weights, f32[768,128]{1,0:T(8,128)S(1)} %shard_map.67.own_ref, f32[768,128]{1,0:T(8,128)S(1)} %collective-permute-done.1.other_ref), custom_call_target="tpu_custom_call" | custom-call | tf_op jit(solution)/shard_map/pallas_call | solution.py:316
  56.3 20.7 %all_to_all.11 = f32[64,1,1536]{2,1,0:T(1,128)S(1)} all-to-all(f32[64,1,1536]{2,1,0:T(1,128)S(1)} %bitcast.8), channel_id=1, replica_groups=mesh['z1'=2,'z0'=2,'y1'=2,'y0'=2,'x1'=2,'x0'=2,'zh'=2,'c'=2] {'z1','z0',..., dimensions={0} | all-to-all | bytes 786432 | tf_op jit(solution)/shard_map/all_to_all | solution.py:260
  77.0 1.7 %shard_map.69 = f32[64,3072]{1,0:T(8,128)} custom-call(f32[768,128]{1,0:T(8,128)S(1)} %bitcast.9, bf16[24,128,128]{2,1,0:T(8,128)(2,1)S(1)} %get-tuple-element.34.weights), custom_call_target="tpu_custom_call" | custom-call | tf_op jit(solution)/shard_map/pallas_call | solution.py:317
  (1 shorter events, 0.0 us)
Async XLA Ops:
  0.0 7.1 %copy-start = (f32[8,8,64,64]{3,2,1,0:T(8,128)S(1)}, f32[8,8,64,64]{3,2,1,0:T(8,128)}, u32[]{:S(2)}) copy-start(f32[8,8,64,64]{3,2,1,0:T(8,128)} %tables.2) | copy-start | bytes 3145732
  0.0 7.1 %copy-start.3 = (s32[8,24,4]{1,2,0:T(4,128)S(1)}, s32[8,24,4]{1,2,0:T(4,128)}, u32[]{:S(2)}) copy-start(s32[8,24,4]{1,2,0:T(4,128)} %param.11) | copy-start | bytes 9220
  0.0 7.1 %copy-start.2 = (s32[8,24,4]{1,2,0:T(4,128)S(1)}, s32[8,24,4]{1,2,0:T(4,128)}, u32[]{:S(2)}) copy-start(s32[8,24,4]{1,2,0:T(4,128)} %param.10) | copy-start | bytes 9220
  0.0 7.1 %copy-start.1 = (f32[24,128,64]{1,2,0:T(8,128)S(1)}, f32[24,128,64]{1,2,0:T(8,128)}, u32[]{:S(2)}) copy-start(f32[24,128,64]{1,2,0:T(8,128)} %param.8) | copy-start | bytes 2359300
  4.9 10.2 %collective-permute-start = (f32[768,128]{1,0:T(8,128)}, f32[768,128]{1,0:T(8,128)S(1)}, u32[]{:S(2)}, u32[]{:S(2)}) collective-permute-start(f32[768,128]{1,0:T(8,128)} %get-tuple-element.25), channel_id=1, source_target_pairs={{0,16},{16,0},{1,17},{17,1},{2,18},{18,2},{3,19},{19,3},{4,20},{20... | collective-permute-start | bytes 1179656 | tf_op jit(solution)/shard_map/ppermute | solution.py:264
  7.1 1.0 %copy-start.4 = (bf16[24,64,128]{2,1,0:T(8,128)(2,1)S(1)}, bf16[24,64,128]{2,1,0:T(8,128)(2,1)}, u32[]{:S(2)}) copy-start(bf16[24,64,128]{2,1,0:T(8,128)(2,1)} %get-tuple-element.23.held) | copy-start | bytes 1179652
  48.1 4.9 %collective-permute-start.1 = (f32[768,128]{1,0:T(8,128)S(1)}, f32[768,128]{1,0:T(8,128)S(1)}, u32[]{:S(2)}, u32[]{:S(2)}) collective-permute-start(f32[768,128]{1,0:T(8,128)S(1)} %get-tuple-element.33), channel_id=1, source_target_pairs={{0,1},{1,0},{2,3},{3,2},{4,5},{5,4},{6,7},{7,6},{8,9},{9,8},{10,11... | collective-permute-start | bytes 1179656 | tf_op jit(solution)/shard_map/ppermute | solution.py:264

commit v8 on v7

--- a/solution.py
+++ b/solution.py
@@ -233,7 +233,7 @@
             out_ref[:, pl.ds(pl.multiple_of(block * width, width), width)] = out
         return carry
 
-    lax.fori_loop(0, blocks // 2, body, 0, unroll=4)
+    lax.fori_loop(0, blocks // 2, body, 0, unroll=True)
 
 
 VMEM = pl.BlockSpec(memory_space=pltpu.VMEM)

time: 79 us -> 78.6 us (level)
  no operation moved by 1% of the time
where the time goes in v8:
time: 78.6 us; the launch traced here: 78.3 us
  blocking collectives  50.1 us (64%)
  Pallas kernels  17.8 us (23%)
  starting transfers between devices  5.6 us (7%)
  waiting for transfers between devices  3.66 us (5%)
  local copies, waits for them, and re-layouts  1 us (1%)
    all_to_all x2, blocking collectives, exchange(): return lax.all_to_all(x, GROUP, 0, 0, tiled=True).reshape(rows, LANES)  50.1 us
    ppermute x2, starting transfers between devices, partner(): return lax.ppermute(x, axis, [(0, 1), (1, 0)])  5.6 us
    pallas_call x1, Pallas kernels, local(): call(start_kernel, [flat, jax.ShapeDtypeStruct((blocks, waves, LANES), BF...  4.87 us
    ppermute x2, waiting for transfers between devices, partner(): return lax.ppermute(x, axis, [(0, 1), (1, 0)])  3.66 us
    pallas_call x1, Pallas kernels, local(): call(middle_kernel, [flat, jax.ShapeDtypeStruct((blocks, waves, LANES), B...  3.6 us
    pallas_call x1, Pallas kernels, local(): call(prepare_kernel, [flat, prepared(4), prepared(3), jax.ShapeDtypeStruc...  3.32 us
    pallas_call x1, Pallas kernels, local(): call(end_kernel, [flat], [SMEM, SMEM, VMEM, VMEM, VMEM], [held, held])  3.23 us
  transfers between devices with their start and end apart: 2, of which 1 were waited for; matrix products, arithmetic and copies ran while one was open for 0% of the time, Pallas kernels for 6%

profile of v8, /device:TPU:1, one launch (start us, length us, event | category | flops | bytes accessed | tf_op | source)
XLA Modules:
  0.0 78.3 jit_solution(5774603515695082957)
XLA Ops:
  0.0 0.0 copy-start
  0.0 0.0 copy-start.3
  0.0 0.0 copy-start.2
  0.0 0.0 copy-start.1
  0.0 4.9 %shard_map.64 = (f32[768,128]{1,0:T(8,128)}, bf16[24,64,128]{2,1,0:T(8,128)(2,1)}) custom-call(s32[8,4,24]{2,1,0:T(4,128)} %bitcast.11, s32[8,4,24]{2,1,0:T(4,128)} %bitcast.16, f32[8,8,64,64]{3,2,1,0:T(8,128)} %tables.2, f32[64,3072]{1,0:T(8,128)} %signals.1, f32[24,64,128]{2,1,0:T(8,128)} %maps.1), custom_call_target="tpu_custom_call" | custom-call | tf_op jit(solution)/shard_map/pallas_call | solution.py:275
  4.9 2.2 %collective-permute-start = (f32[768,128]{1,0:T(8,128)}, f32[768,128]{1,0:T(8,128)S(1)}, u32[]{:S(2)}, u32[]{:S(2)}) collective-permute-start(f32[768,128]{1,0:T(8,128)} %get-tuple-element.25), channel_id=1, source_target_pairs={{0,16},{16,0},{1,17},{17,1},{2,18},{18,2},{3,19},{19,3},{4,20},{20... | collective-permute-start | bytes 1179656 | tf_op jit(solution)/shard_map/ppermute | solution.py:264
  7.1 0.0 copy-done
  7.1 0.0 copy-done.3
  7.1 0.0 copy-done.2
  7.1 0.0 copy-done.1
  7.1 0.0 copy-start.4
  7.1 1.0 %copy-done.4 = bf16[24,64,128]{2,1,0:T(8,128)(2,1)S(1)} copy-done((bf16[24,64,128]{2,1,0:T(8,128)(2,1)S(1)}, bf16[24,64,128]{2,1,0:T(8,128)(2,1)}, u32[]{:S(2)}) %copy-start.4) | copy-done | bytes 393240
  8.1 3.3 %shard_map.65 = (f32[768,128]{1,0:T(8,128)S(1)}, bf16[4,8,64,128]{3,2,1,0:T(8,128)(2,1)S(1)}, bf16[3,8,64,128]{3,2,1,0:T(8,128)(2,1)S(1)}, bf16[24,128,128]{2,1,0:T(8,128)(2,1)S(1)}) custom-call(s32[8,4,24]{2,1,0:T(4,128)S(1)} %bitcast.12, s32[8,4,24]{2,1,0:T(4,128)S(1)} %bitcast.17, f32[8,8,64,64]{3,2,1,0:T(8,128)S(1)} %copy-done, ...), custom_call_target="tpu_custom_call" | custom-call | flops 16777216 | bytes 8388608 | tf_op jit(solution)/shard_map/pallas_call | solution.py:294
  11.4 3.7 %collective-permute-done = f32[768,128]{1,0:T(8,128)S(1)} collective-permute-done((f32[768,128]{1,0:T(8,128)}, f32[768,128]{1,0:T(8,128)S(1)}, u32[]{:S(2)}, u32[]{:S(2)}) %collective-permute-start) | collective-permute-done | bytes 393248 | tf_op jit(solution)/shard_map/ppermute | solution.py:264
  15.1 29.4 %all_to_all.10 = f32[64,1,1536]{2,1,0:T(1,128)S(1)} all-to-all(f32[64,1,1536]{2,1,0:T(1,128)S(1)} %bitcast.21), channel_id=1, replica_groups=mesh['z1'=2,'z0'=2,'y1'=2,'y0'=2,'x1'=2,'x0'=2,'zh'=2,'c'=2] {'z1','z0',..., dimensions={0} | all-to-all | bytes 786432 | tf_op jit(solution)/shard_map/all_to_all | solution.py:260
  44.5 3.6 %shard_map.66 = (f32[768,128]{1,0:T(8,128)S(1)}, bf16[24,64,128]{2,1,0:T(8,128)(2,1)S(1)}) custom-call(s32[8,4,24]{2,1,0:T(4,128)S(1)} %bitcast.13, s32[8,4,24]{2,1,0:T(4,128)S(1)} %bitcast.18, bf16[4,8,64,128]{3,2,1,0:T(8,128)(2,1)S(1)} %get-tuple-element.30.weights, f32[768,128]{1,0:T(8,128)S(1)} %bitcast.7), custom_call_target="tpu_custom_call" | custom-call | tf_op jit(solution)/shard_map/pallas_call | solution.py:303
  48.1 3.4 %collective-permute-start.1 = (f32[768,128]{1,0:T(8,128)S(1)}, f32[768,128]{1,0:T(8,128)S(1)}, u32[]{:S(2)}, u32[]{:S(2)}) collective-permute-start(f32[768,128]{1,0:T(8,128)S(1)} %get-tuple-element.33), channel_id=1, source_target_pairs={{0,1},{1,0},{2,3},{3,2},{4,5},{5,4},{6,7},{7,6},{8,9},{9,8},{10,11... | collective-permute-start | bytes 1179656 | tf_op jit(solution)/shard_map/ppermute | solution.py:264
  51.5 1.5 %shard_map.67.own_ref = f32[768,128]{1,0:T(8,128)S(1)} custom-call(s32[8,4,24]{2,1,0:T(4,128)S(1)} %bitcast.14, s32[8,4,24]{2,1,0:T(4,128)S(1)} %bitcast.19, bf16[4,8,64,128]{3,2,1,0:T(8,128)(2,1)S(1)} %get-tuple-element.30.weights, bf16[24,64,128]{2,1,0:T(8,128)(2,1)S(1)} %get-tuple-element.32.left), custom_call_target="tpu_custom_call" | custom-call | flops 16777216 | bytes 1048576 | tf_op jit(solution)/shard_map/pallas_call | solution.py:310
  53.0 0.0 collective-permute-done.1.other_ref
  53.0 3.2 %shard_map.68 = f32[768,128]{1,0:T(8,128)S(1)} custom-call(s32[8,4,24]{2,1,0:T(4,128)S(1)} %bitcast.15, s32[8,4,24]{2,1,0:T(4,128)S(1)} %bitcast.20, bf16[3,8,64,128]{3,2,1,0:T(8,128)(2,1)S(1)} %get-tuple-element.29.weights, f32[768,128]{1,0:T(8,128)S(1)} %shard_map.67.own_ref, f32[768,128]{1,0:T(8,128)S(1)} %collective-permute-done.1.other_ref), custom_call_target="tpu_custom_call" | custom-call | tf_op jit(solution)/shard_map/pallas_call | solution.py:316
  56.3 20.7 %all_to_all.11 = f32[64,1,1536]{2,1,0:T(1,128)S(1)} all-to-all(f32[64,1,1536]{2,1,0:T(1,128)S(1)} %bitcast.8), channel_id=1, replica_groups=mesh['z1'=2,'z0'=2,'y1'=2,'y0'=2,'x1'=2,'x0'=2,'zh'=2,'c'=2] {'z1','z0',..., dimensions={0} | all-to-all | bytes 786432 | tf_op jit(solution)/shard_map/all_to_all | solution.py:260
  77.0 1.3 %shard_map.69 = f32[64,3072]{1,0:T(8,128)} custom-call(f32[768,128]{1,0:T(8,128)S(1)} %bitcast.9, bf16[24,128,128]{2,1,0:T(8,128)(2,1)S(1)} %get-tuple-element.34.weights), custom_call_target="tpu_custom_call" | custom-call | tf_op jit(solution)/shard_map/pallas_call | solution.py:317
  (1 shorter events, 0.0 us)
Async XLA Ops:
  0.0 7.1 %copy-start = (f32[8,8,64,64]{3,2,1,0:T(8,128)S(1)}, f32[8,8,64,64]{3,2,1,0:T(8,128)}, u32[]{:S(2)}) copy-start(f32[8,8,64,64]{3,2,1,0:T(8,128)} %tables.2) | copy-start | bytes 3145732
  0.0 7.1 %copy-start.3 = (s32[8,24,4]{1,2,0:T(4,128)S(1)}, s32[8,24,4]{1,2,0:T(4,128)}, u32[]{:S(2)}) copy-start(s32[8,24,4]{1,2,0:T(4,128)} %param.11) | copy-start | bytes 9220
  0.0 7.1 %copy-start.2 = (s32[8,24,4]{1,2,0:T(4,128)S(1)}, s32[8,24,4]{1,2,0:T(4,128)}, u32[]{:S(2)}) copy-start(s32[8,24,4]{1,2,0:T(4,128)} %param.10) | copy-start | bytes 9220
  0.0 7.1 %copy-start.1 = (f32[24,128,64]{1,2,0:T(8,128)S(1)}, f32[24,128,64]{1,2,0:T(8,128)}, u32[]{:S(2)}) copy-start(f32[24,128,64]{1,2,0:T(8,128)} %param.8) | copy-start | bytes 2359300
  4.9 10.2 %collective-permute-start = (f32[768,128]{1,0:T(8,128)}, f32[768,128]{1,0:T(8,128)S(1)}, u32[]{:S(2)}, u32[]{:S(2)}) collective-permute-start(f32[768,128]{1,0:T(8,128)} %get-tuple-element.25), channel_id=1, source_target_pairs={{0,16},{16,0},{1,17},{17,1},{2,18},{18,2},{3,19},{19,3},{4,20},{20... | collective-permute-start | bytes 1179656 | tf_op jit(solution)/shard_map/ppermute | solution.py:264
  7.1 1.0 %copy-start.4 = (bf16[24,64,128]{2,1,0:T(8,128)(2,1)S(1)}, bf16[24,64,128]{2,1,0:T(8,128)(2,1)}, u32[]{:S(2)}) copy-start(bf16[24,64,128]{2,1,0:T(8,128)(2,1)} %get-tuple-element.23.held) | copy-start | bytes 1179652
  48.1 4.9 %collective-permute-start.1 = (f32[768,128]{1,0:T(8,128)S(1)}, f32[768,128]{1,0:T(8,128)S(1)}, u32[]{:S(2)}, u32[]{:S(2)}) collective-permute-start(f32[768,128]{1,0:T(8,128)S(1)} %get-tuple-element.33), channel_id=1, source_target_pairs={{0,1},{1,0},{2,3},{3,2},{4,5},{5,4},{6,7},{7,6},{8,9},{9,8},{10,11... | collective-permute-start | bytes 1179656 | tf_op jit(solution)/shard_map/ppermute | solution.py:264

commit v9 on v8

--- a/solution.py
+++ b/solution.py
@@ -281,7 +281,7 @@
             pltpu.VMEM((kinds, rank, rank), F32),
             pltpu.VMEM((waves, blocks * width), F32),
             pltpu.VMEM((blocks, rank, width), F32),
-            pltpu.SemaphoreType.DMA((3, 3)),
+            pltpu.SemaphoreType.DMA((3, 6)),
         ],
         mib=60,
     )(sources, types, translations, signals, leaf_maps)

time: 78.6 us -> 79.3 us (level)
  no operation moved by 1% of the time
where the time goes in v9:
time: 79.3 us; the launch traced here: 79 us
  blocking collectives  50 us (63%)
  Pallas kernels  18.5 us (23%)
  starting transfers between devices  5.7 us (7%)
  waiting for transfers between devices  3.66 us (5%)
  local copies, waits for them, and re-layouts  1 us (1%)
    all_to_all x2, blocking collectives, exchange(): return lax.all_to_all(x, GROUP, 0, 0, tiled=True).reshape(rows, LANES)  50 us
    ppermute x2, starting transfers between devices, partner(): return lax.ppermute(x, axis, [(0, 1), (1, 0)])  5.7 us
    pallas_call x1, Pallas kernels, local(): call(start_kernel, [flat, jax.ShapeDtypeStruct((blocks, waves, LANES), BF...  5.53 us
    ppermute x2, waiting for transfers between devices, partner(): return lax.ppermute(x, axis, [(0, 1), (1, 0)])  3.66 us
    pallas_call x1, Pallas kernels, local(): call(middle_kernel, [flat, jax.ShapeDtypeStruct((blocks, waves, LANES), B...  3.6 us
    pallas_call x1, Pallas kernels, local(): call(prepare_kernel, [flat, prepared(4), prepared(3), jax.ShapeDtypeStruc...  3.32 us
    pallas_call x1, Pallas kernels, local(): call(end_kernel, [flat], [SMEM, SMEM, VMEM, VMEM, VMEM], [held, held])  3.22 us
  transfers between devices with their start and end apart: 2, of which 1 were waited for; matrix products, arithmetic and copies ran while one was open for 0% of the time, Pallas kernels for 6%

profile of v9, /device:TPU:1, one launch (start us, length us, event | category | flops | bytes accessed | tf_op | source)
XLA Modules:
  0.0 79.0 jit_solution(5094502118305602342)
XLA Ops:
  0.0 0.0 copy-start
  0.0 0.0 copy-start.3
  0.0 0.0 copy-start.2
  0.0 0.0 copy-start.1
  0.0 5.5 %shard_map.64 = (f32[768,128]{1,0:T(8,128)}, bf16[24,64,128]{2,1,0:T(8,128)(2,1)}) custom-call(s32[8,4,24]{2,1,0:T(4,128)} %bitcast.11, s32[8,4,24]{2,1,0:T(4,128)} %bitcast.16, f32[8,8,64,64]{3,2,1,0:T(8,128)} %tables.2, f32[64,3072]{1,0:T(8,128)} %signals.1, f32[24,64,128]{2,1,0:T(8,128)} %maps.1), custom_call_target="tpu_custom_call" | custom-call | tf_op jit(solution)/shard_map/pallas_call | solution.py:275
  5.6 2.2 %collective-permute-start = (f32[768,128]{1,0:T(8,128)}, f32[768,128]{1,0:T(8,128)S(1)}, u32[]{:S(2)}, u32[]{:S(2)}) collective-permute-start(f32[768,128]{1,0:T(8,128)} %get-tuple-element.25), channel_id=1, source_target_pairs={{0,16},{16,0},{1,17},{17,1},{2,18},{18,2},{3,19},{19,3},{4,20},{20... | collective-permute-start | bytes 1179656 | tf_op jit(solution)/shard_map/ppermute | solution.py:264
  7.8 0.0 copy-done
  7.8 0.0 copy-done.3
  7.8 0.0 copy-done.2
  7.8 0.0 copy-done.1
  7.8 0.0 copy-start.4
  7.8 1.0 %copy-done.4 = bf16[24,64,128]{2,1,0:T(8,128)(2,1)S(1)} copy-done((bf16[24,64,128]{2,1,0:T(8,128)(2,1)S(1)}, bf16[24,64,128]{2,1,0:T(8,128)(2,1)}, u32[]{:S(2)}) %copy-start.4) | copy-done | bytes 393240
  8.8 3.3 %shard_map.65 = (f32[768,128]{1,0:T(8,128)S(1)}, bf16[4,8,64,128]{3,2,1,0:T(8,128)(2,1)S(1)}, bf16[3,8,64,128]{3,2,1,0:T(8,128)(2,1)S(1)}, bf16[24,128,128]{2,1,0:T(8,128)(2,1)S(1)}) custom-call(s32[8,4,24]{2,1,0:T(4,128)S(1)} %bitcast.12, s32[8,4,24]{2,1,0:T(4,128)S(1)} %bitcast.17, f32[8,8,64,64]{3,2,1,0:T(8,128)S(1)} %copy-done, ...), custom_call_target="tpu_custom_call" | custom-call | flops 16777216 | bytes 8388608 | tf_op jit(solution)/shard_map/pallas_call | solution.py:294
  12.1 3.7 %collective-permute-done = f32[768,128]{1,0:T(8,128)S(1)} collective-permute-done((f32[768,128]{1,0:T(8,128)}, f32[768,128]{1,0:T(8,128)S(1)}, u32[]{:S(2)}, u32[]{:S(2)}) %collective-permute-start) | collective-permute-done | bytes 393248 | tf_op jit(solution)/shard_map/ppermute | solution.py:264
  15.8 29.3 %all_to_all.10 = f32[64,1,1536]{2,1,0:T(1,128)S(1)} all-to-all(f32[64,1,1536]{2,1,0:T(1,128)S(1)} %bitcast.21), channel_id=1, replica_groups=mesh['z1'=2,'z0'=2,'y1'=2,'y0'=2,'x1'=2,'x0'=2,'zh'=2,'c'=2] {'z1','z0',..., dimensions={0} | all-to-all | bytes 786432 | tf_op jit(solution)/shard_map/all_to_all | solution.py:260
  45.1 3.6 %shard_map.66 = (f32[768,128]{1,0:T(8,128)S(1)}, bf16[24,64,128]{2,1,0:T(8,128)(2,1)S(1)}) custom-call(s32[8,4,24]{2,1,0:T(4,128)S(1)} %bitcast.13, s32[8,4,24]{2,1,0:T(4,128)S(1)} %bitcast.18, bf16[4,8,64,128]{3,2,1,0:T(8,128)(2,1)S(1)} %get-tuple-element.30.weights, f32[768,128]{1,0:T(8,128)S(1)} %bitcast.7), custom_call_target="tpu_custom_call" | custom-call | tf_op jit(solution)/shard_map/pallas_call | solution.py:303
  48.7 3.5 %collective-permute-start.1 = (f32[768,128]{1,0:T(8,128)S(1)}, f32[768,128]{1,0:T(8,128)S(1)}, u32[]{:S(2)}, u32[]{:S(2)}) collective-permute-start(f32[768,128]{1,0:T(8,128)S(1)} %get-tuple-element.33), channel_id=1, source_target_pairs={{0,1},{1,0},{2,3},{3,2},{4,5},{5,4},{6,7},{7,6},{8,9},{9,8},{10,11... | collective-permute-start | bytes 1179656 | tf_op jit(solution)/shard_map/ppermute | solution.py:264
  52.2 1.5 %shard_map.67.own_ref = f32[768,128]{1,0:T(8,128)S(1)} custom-call(s32[8,4,24]{2,1,0:T(4,128)S(1)} %bitcast.14, s32[8,4,24]{2,1,0:T(4,128)S(1)} %bitcast.19, bf16[4,8,64,128]{3,2,1,0:T(8,128)(2,1)S(1)} %get-tuple-element.30.weights, bf16[24,64,128]{2,1,0:T(8,128)(2,1)S(1)} %get-tuple-element.32.left), custom_call_target="tpu_custom_call" | custom-call | flops 16777216 | bytes 1048576 | tf_op jit(solution)/shard_map/pallas_call | solution.py:310
  53.7 0.0 collective-permute-done.1.other_ref
  53.7 3.2 %shard_map.68 = f32[768,128]{1,0:T(8,128)S(1)} custom-call(s32[8,4,24]{2,1,0:T(4,128)S(1)} %bitcast.15, s32[8,4,24]{2,1,0:T(4,128)S(1)} %bitcast.20, bf16[3,8,64,128]{3,2,1,0:T(8,128)(2,1)S(1)} %get-tuple-element.29.weights, f32[768,128]{1,0:T(8,128)S(1)} %shard_map.67.own_ref, f32[768,128]{1,0:T(8,128)S(1)} %collective-permute-done.1.other_ref), custom_call_target="tpu_custom_call" | custom-call | tf_op jit(solution)/shard_map/pallas_call | solution.py:316
  56.9 20.7 %all_to_all.11 = f32[64,1,1536]{2,1,0:T(1,128)S(1)} all-to-all(f32[64,1,1536]{2,1,0:T(1,128)S(1)} %bitcast.8), channel_id=1, replica_groups=mesh['z1'=2,'z0'=2,'y1'=2,'y0'=2,'x1'=2,'x0'=2,'zh'=2,'c'=2] {'z1','z0',..., dimensions={0} | all-to-all | bytes 786432 | tf_op jit(solution)/shard_map/all_to_all | solution.py:260
  77.7 1.3 %shard_map.69 = f32[64,3072]{1,0:T(8,128)} custom-call(f32[768,128]{1,0:T(8,128)S(1)} %bitcast.9, bf16[24,128,128]{2,1,0:T(8,128)(2,1)S(1)} %get-tuple-element.34.weights), custom_call_target="tpu_custom_call" | custom-call | tf_op jit(solution)/shard_map/pallas_call | solution.py:317
  (1 shorter events, 0.0 us)
Async XLA Ops:
  0.0 7.8 %copy-start = (f32[8,8,64,64]{3,2,1,0:T(8,128)S(1)}, f32[8,8,64,64]{3,2,1,0:T(8,128)}, u32[]{:S(2)}) copy-start(f32[8,8,64,64]{3,2,1,0:T(8,128)} %tables.2) | copy-start | bytes 3145732
  0.0 7.8 %copy-start.3 = (s32[8,24,4]{1,2,0:T(4,128)S(1)}, s32[8,24,4]{1,2,0:T(4,128)}, u32[]{:S(2)}) copy-start(s32[8,24,4]{1,2,0:T(4,128)} %param.11) | copy-start | bytes 9220
  0.0 7.8 %copy-start.2 = (s32[8,24,4]{1,2,0:T(4,128)S(1)}, s32[8,24,4]{1,2,0:T(4,128)}, u32[]{:S(2)}) copy-start(s32[8,24,4]{1,2,0:T(4,128)} %param.10) | copy-start | bytes 9220
  0.0 7.8 %copy-start.1 = (f32[24,128,64]{1,2,0:T(8,128)S(1)}, f32[24,128,64]{1,2,0:T(8,128)}, u32[]{:S(2)}) copy-start(f32[24,128,64]{1,2,0:T(8,128)} %param.8) | copy-start | bytes 2359300
  5.6 10.2 %collective-permute-start = (f32[768,128]{1,0:T(8,128)}, f32[768,128]{1,0:T(8,128)S(1)}, u32[]{:S(2)}, u32[]{:S(2)}) collective-permute-start(f32[768,128]{1,0:T(8,128)} %get-tuple-element.25), channel_id=1, source_target_pairs={{0,16},{16,0},{1,17},{17,1},{2,18},{18,2},{3,19},{19,3},{4,20},{20... | collective-permute-start | bytes 1179656 | tf_op jit(solution)/shard_map/ppermute | solution.py:264
  7.8 1.0 %copy-start.4 = (bf16[24,64,128]{2,1,0:T(8,128)(2,1)S(1)}, bf16[24,64,128]{2,1,0:T(8,128)(2,1)}, u32[]{:S(2)}) copy-start(bf16[24,64,128]{2,1,0:T(8,128)(2,1)} %get-tuple-element.23.held) | copy-start | bytes 1179652
  48.7 5.0 %collective-permute-start.1 = (f32[768,128]{1,0:T(8,128)S(1)}, f32[768,128]{1,0:T(8,128)S(1)}, u32[]{:S(2)}, u32[]{:S(2)}) collective-permute-start(f32[768,128]{1,0:T(8,128)S(1)} %get-tuple-element.33), channel_id=1, source_target_pairs={{0,1},{1,0},{2,3},{3,2},{4,5},{5,4},{6,7},{7,6},{8,9},{9,8},{10,11... | collective-permute-start | bytes 1179656 | tf_op jit(solution)/shard_map/ppermute | solution.py:264
